TPU v7x, 32 devices: a whole 2x2x4 slice. The times are simulated.
32 devices in a mesh: member: 8 (over z, y), region: 4 (over x, core).
Axes of the slice: x: 2, y: 2, z: 4, core: 2. Of those that a mesh axis runs over, the one named last changes fastest.
Arguments:
- background_realizations: float32 [1024, 32768], P('member', 'region'), may hold values from -6 to 6
- realization_expected_data: float32 [1024, 16384], P('member', 'region'), may hold values from -6 to 6
- departure_values: float32 [1024, 16384], P('member', 'region'), may hold values from -6 to 6
- instrument_dispersion: float32 [16384], P('region'), may hold values from 0.5 to 2
- window_piece_offsets: int32 [4, 9], P('region'), may hold values from 0 to 64, as said below
- window_data_pieces: int32 [4, 8, 4], P('region'), may hold values from 0 to 39, as said below
- neighbor_piece_ids: int32 [4, 2, 4], P('region'), may hold values from 0 to 31, as said below
- coupling_indicator: int32 [4, 64, 4], P('region'), may hold values 0 or 1
Outputs:
- analysis: float32 [1024, 32768], P('member', 'region')
Inputs may be any that keep to these rules, and one draw needn't show every extreme that they name: `window_piece_offsets`: each row starts at 0, ends at 64 and rises by 1 or more at each entry; entry p lies within 3 of p * 8; in every row one patch spans exactly 14 blocks. `window_data_pieces`: entries index a region's extended observation blocks: 0 to 31 its own, then 4 received from the region before it, then 4 from the region after it; the 4 entries of a patch differ. `neighbor_piece_ids`: entries index the sending region's own observation blocks; the 4 entries of a row differ.
All inputs are finite; a program needn't handle non-finite values. No bound on the sum of `coupling_indicator` on one device may be relied on, other than what follows from the above.
Results may differ from a plain program's by a relative error of at most 0.0003.
Values sent between devices are 32-bit elements; how exact they have to be, the bound alone decides.
A program may use at most 128 MiB of HBM per device.

v0:
```python
import functools

import jax
import jax.numpy as jnp
from jax import lax
from jax.experimental import pallas as pl
from jax.experimental.pallas import tpu as pltpu
from jax.sharding import PartitionSpec as P

PIECE_LENGTH = 128
OBS_PER = 4
LOCAL = 512


highest = lax.Precision.HIGHEST
high = lax.Precision.HIGH


def shifted(block, axis, distance):
    count = lax.axis_size(axis)
    return lax.ppermute(block, axis, [(i, (i + distance) % count) for i in range(count)])


def pieces(start, count=1):
    return pl.ds(pl.multiple_of(start * PIECE_LENGTH, PIECE_LENGTH), count * PIECE_LENGTH)


def halo_kernel(ids_ref, expected_ref, innov_ref, after_ref, before_ref):
    count = ids_ref.shape[1]
    for side, out_ref in ((0, after_ref), (1, before_ref)):
        for k in range(count):
            source = pieces(ids_ref[side, k])
            out_ref[:, k * PIECE_LENGTH : (k + 1) * PIECE_LENGTH] = expected_ref[:, source]
            out_ref[:, (count + k) * PIECE_LENGTH : (count + k + 1) * PIECE_LENGTH] = innov_ref[:, source]


def halo_pack(ids, expected, innov):
    rows = expected.shape[0]
    shape = jax.ShapeDtypeStruct((rows, 2 * ids.shape[1] * PIECE_LENGTH), jnp.float32)
    return pl.pallas_call(
        halo_kernel,
        out_shape=(shape, shape),
        in_specs=[
            pl.BlockSpec(memory_space=pltpu.SMEM),
            pl.BlockSpec(memory_space=pltpu.VMEM),
            pl.BlockSpec(memory_space=pltpu.VMEM),
        ],
        out_specs=(pl.BlockSpec(memory_space=pltpu.VMEM),) * 2,
        name="halo_pack",
    )(ids, expected, innov)


def window_kernel(half, lists_ref, own_ref, before_ref, after_ref, out_ref):
    rows, width = own_ref.shape
    own_count = width // PIECE_LENGTH
    side = before_ref.shape[1] // (2 * PIECE_LENGTH)
    patches, per = lists_ref.shape

    @pl.loop(0, patches)
    def _(p):
        base = pl.multiple_of(p * rows, rows)
        for k in range(per):
            entry = lists_ref[p, k]
            target = (pl.ds(base, rows), slice(k * PIECE_LENGTH, (k + 1) * PIECE_LENGTH))

            @pl.when(entry < own_count)
            def _():
                out_ref[target] = own_ref[:, pieces(entry)]

            @pl.when((entry >= own_count) & (entry < own_count + side))
            def _():
                out_ref[target] = before_ref[:, pieces(entry - own_count + half * side)]

            @pl.when(entry >= own_count + side)
            def _():
                out_ref[target] = after_ref[:, pieces(entry - own_count - side + half * side)]


def window_pack(half, lists, own, before, after):
    rows = own.shape[0]
    patches, per = lists.shape
    return pl.pallas_call(
        functools.partial(window_kernel, half),
        out_shape=jax.ShapeDtypeStruct((patches * rows, per * PIECE_LENGTH), jnp.float32),
        in_specs=[pl.BlockSpec(memory_space=pltpu.SMEM)]
        + [pl.BlockSpec(memory_space=pltpu.VMEM)] * 3,
        out_specs=pl.BlockSpec(memory_space=pltpu.VMEM),
        name="window_pack",
    )(lists, own, before, after)


def to_owners(rows_by_owner):
    return lax.all_to_all(rows_by_owner, "member", split_axis=0, concat_axis=0, tiled=True)


def snake(index, row):
    return index + (index // row) % 2 * (row - 1 - 2 * (index % row))


def split_kernel(in_ref, first_ref, second_ref):
    half = first_ref.shape[1]
    first_ref[...] = in_ref[:, :half]
    second_ref[...] = in_ref[:, half:]


def state_pack(background, groups, row, half):
    rows, total = background.shape
    width = total // groups
    return pl.pallas_call(
        split_kernel,
        grid=(groups,),
        out_shape=(
            jax.ShapeDtypeStruct((groups * rows, half), jnp.float32),
            jax.ShapeDtypeStruct((groups * rows, width - half), jnp.float32),
        ),
        in_specs=[pl.BlockSpec((rows, width), lambda i: (0, snake(i, row)))],
        out_specs=(
            pl.BlockSpec((rows, half), lambda i: (i, 0)),
            pl.BlockSpec((rows, width - half), lambda i: (i, 0)),
        ),
        name="state_pack",
    )(background)


def join_kernel(edge, centre_ref, sides_ref, out_ref):
    width = out_ref.shape[1]
    out_ref[:, :edge] = sides_ref[:, :edge]
    out_ref[:, edge : width - edge] = centre_ref[...]
    out_ref[:, width - edge :] = sides_ref[:, edge:]


def state_join(centre, sides, groups, row):
    rows = centre.shape[0] // groups
    edge = sides.shape[1] // 2
    width = centre.shape[1] + 2 * edge
    return pl.pallas_call(
        functools.partial(join_kernel, edge),
        grid=(groups,),
        out_shape=jax.ShapeDtypeStruct((rows, groups * width), jnp.float32),
        in_specs=[
            pl.BlockSpec((rows, width - 2 * edge), lambda i: (i, 0)),
            pl.BlockSpec((rows, 2 * edge), lambda i: (i, 0)),
        ],
        out_specs=pl.BlockSpec((rows, width), lambda i: (0, snake(i, row))),
        name="state_join",
    )(centre, sides)


def masked_gain(states, perturbed, cover_rows):
    realization_records, row_count = states.shape
    centred = states - jnp.mean(states, axis=0, keepdims=True)
    gain = lax.dot_general(
        centred,
        perturbed,
        (((0,), (0,)), ((), ())),
        precision=high,
        preferred_element_type=jnp.float32,
    ) / (realization_records - 1.0)
    cover = jnp.repeat(jnp.repeat(cover_rows, PIECE_LENGTH, axis=1), PIECE_LENGTH, axis=0)
    return gain * cover


def times_transposed(left, right, precision=high):
    return lax.dot_general(
        left,
        right,
        (((1,), (1,)), ((), ())),
        precision=precision,
        preferred_element_type=jnp.float32,
    )


def factor_kernel(block_ref, inverse_ref, work_ref):
    size = block_ref.shape[0]
    wide = 2 * size
    eye = lax.broadcasted_iota(jnp.int32, (size, size), 0) == lax.broadcasted_iota(
        jnp.int32, (size, size), 1
    )
    work_ref[:, :size] = block_ref[...]
    work_ref[:, size:] = eye.astype(jnp.float32)
    step_rows = 8
    row_ids = lax.broadcasted_iota(jnp.int32, (step_rows, wide), 0)
    for start in range(0, size, step_rows):
        rows = work_ref[start : start + step_rows, :]
        for j in range(step_rows):
            column = rows[:, start + j : start + j + 1]
            scale = 1.0 / jnp.sqrt(column[j : j + 1, :])
            pivot = rows[j : j + 1, :] * scale
            lowered = rows - (column * scale) * pivot
            rows = jnp.where(row_ids > j, lowered, jnp.where(row_ids == j, pivot, rows))
        inverse_ref[start : start + step_rows, :] = rows[:, size:]
        after = start + step_rows
        if after < size:
            change = lax.dot_general(
                rows[:, :size],
                rows,
                (((0,), (0,)), ((), ())),
                precision=highest,
                preferred_element_type=jnp.float32,
            )
            work_ref[after:, :] = work_ref[after:, :] - change[after:, :]


def factor_block(block):
    size = block.shape[0]
    return pl.pallas_call(
        factor_kernel,
        out_shape=jax.ShapeDtypeStruct((size, size), jnp.float32),
        in_specs=[pl.BlockSpec(memory_space=pltpu.VMEM)],
        out_specs=pl.BlockSpec(memory_space=pltpu.VMEM),
        scratch_shapes=[pltpu.VMEM((size, 2 * size), jnp.float32)],
        name="factor_block",
    )(block)


def factor_step(trailing):
    inverse = factor_block(trailing[:PIECE_LENGTH, :PIECE_LENGTH])
    panel = times_transposed(trailing[PIECE_LENGTH:, :PIECE_LENGTH], inverse, highest)
    rest = trailing[PIECE_LENGTH:, PIECE_LENGTH:] - times_transposed(panel, panel, highest)
    return inverse, panel, rest


def solve_rows(inverses, panels, innovated):
    count = len(inverses)
    rest = innovated
    forward = []
    for k in range(count):
        part = times_transposed(rest[:, :PIECE_LENGTH], inverses[k], highest)
        forward.append(part)
        if k + 1 < count:
            rest = rest[:, PIECE_LENGTH:] - times_transposed(part, panels[k], highest)
    done = None
    for k in reversed(range(count)):
        part = forward[k]
        if done is not None:
            part = part - jnp.dot(
                done, panels[k], precision=highest, preferred_element_type=jnp.float32
            )
        part = jnp.dot(
            part, inverses[k], precision=highest, preferred_element_type=jnp.float32
        )
        done = part if done is None else jnp.concatenate([part, done], axis=1)
    return done


def body(
    row,
    background_realizations,
    realization_expected_data,
    departure_values,
    instrument_dispersion,
    window_piece_offsets,
    window_data_pieces,
    neighbor_piece_ids,
    coupling_indicator,
):
    groups = lax.axis_size("member")
    patch = snake(lax.axis_index("member"), row)
    rows, variable_total = background_realizations.shape
    segment_total = variable_total // PIECE_LENGTH
    per_device = segment_total // groups
    spread = (per_device - 1) // 2
    own_width = per_device * PIECE_LENGTH
    half = per_device // 2 * PIECE_LENGTH
    edge = spread * PIECE_LENGTH
    obs_count = realization_expected_data.shape[1] // PIECE_LENGTH
    lists = window_data_pieces[0]
    sorted_lists = jnp.stack([lists[snake(i, row)] for i in range(groups)])
    halo_ids = neighbor_piece_ids[0]
    up = [(snake(p, row), snake(p + 1, row)) for p in range(groups - 1)]
    down = [(after, before) for before, after in up]

    send_first, send_second = state_pack(background_realizations, groups, row, half)
    first_states = to_owners(send_first)

    after_send, before_send = halo_pack(halo_ids, realization_expected_data, departure_values)
    var_blocks = instrument_dispersion.reshape(obs_count, PIECE_LENGTH)
    from_before = shifted(after_send, "region", 1)
    from_after = shifted(before_send, "region", -1)
    var_before = shifted(jnp.take(var_blocks, halo_ids[0], axis=0), "region", 1)
    var_after = shifted(jnp.take(var_blocks, halo_ids[1], axis=0), "region", -1)
    var_ext = jnp.concatenate([var_blocks, var_before, var_after], axis=0)
    own_list = lax.dynamic_index_in_dim(lists, patch, 0, keepdims=False)
    variance = jnp.take(var_ext, own_list, axis=0).reshape(LOCAL)

    send_expected = window_pack(
        0, sorted_lists, realization_expected_data, from_before, from_after
    )
    send_innov = window_pack(1, sorted_lists, departure_values, from_before, from_after)
    first_states, send_expected, send_innov, variance = lax.optimization_barrier(
        (first_states, send_expected, send_innov, variance)
    )
    expected = to_owners(send_expected)
    expected, send_second, first_states = lax.optimization_barrier(
        (expected, send_second, first_states)
    )
    second_states = to_owners(send_second)
    high_states = lax.ppermute(first_states[:, :edge], "member", down)
    members = first_states.shape[0]

    perturbed = expected - jnp.mean(expected, axis=0, keepdims=True)
    cov_obs = jnp.dot(
        perturbed.T, perturbed, precision=highest, preferred_element_type=jnp.float32
    ) / (members - 1.0)
    trailing = cov_obs + jnp.diag(variance)
    inverses, panels = [], []
    for k in range(OBS_PER):
        if k == OBS_PER // 2:
            trailing, second_states, send_innov = lax.optimization_barrier(
                (trailing, second_states, send_innov)
            )
            innovated = to_owners(send_innov)
            low_states = lax.ppermute(
                second_states[:, own_width - half - edge :], "member", up
            )
        if k + 1 < OBS_PER:
            inverse, panel, trailing = factor_step(trailing)
            panels.append(panel)
        else:
            inverse = factor_block(trailing)
        inverses.append(inverse)
    inverses[-1], innovated = lax.optimization_barrier((inverses[-1], innovated))
    weights = solve_rows(inverses, panels, innovated)

    cover_all = coupling_indicator[0].astype(jnp.float32)
    first = patch * per_device
    cover_pad = jnp.pad(cover_all, ((spread, spread), (0, 0)))
    covers = lax.dynamic_slice_in_dim(cover_pad, first, per_device + 2 * spread, axis=0)
    split = half // PIECE_LENGTH
    low_gain = masked_gain(low_states, perturbed, covers[:spread])
    high_gain = masked_gain(high_states, perturbed, covers[per_device + spread :])
    first_gain = masked_gain(first_states, perturbed, covers[spread : spread + split])
    second_gain = masked_gain(
        second_states, perturbed, covers[spread + split : spread + per_device]
    )
    inc_high = lax.ppermute(times_transposed(weights, low_gain), "member", down)
    inc_low = lax.ppermute(times_transposed(weights, high_gain), "member", up)
    first_inc = times_transposed(weights, first_gain)
    second_inc = times_transposed(weights, second_gain)
    bounds = lax.dynamic_slice_in_dim(window_piece_offsets[0], patch, 2) - first
    block = jnp.arange(own_width) // PIECE_LENGTH
    from_low = (block < bounds[0])[None, :edge]
    from_high = (block >= bounds[1])[None, own_width - edge :]
    tail = own_width - half - edge
    centre = jnp.concatenate(
        [
            first_states[:, edge:] + first_inc[:, edge:],
            second_states[:, :tail] + second_inc[:, :tail],
        ],
        axis=1,
    )
    centre_back = to_owners(centre)
    sides = jnp.concatenate(
        [
            first_states[:, :edge] + jnp.where(from_low, inc_low, first_inc[:, :edge]),
            second_states[:, tail:] + jnp.where(from_high, inc_high, second_inc[:, tail:]),
        ],
        axis=1,
    )
    sides_back = to_owners(sides)
    return state_join(centre_back, sides_back, groups, row)


def row_length(mesh):
    devices = mesh.devices[:, 0].tolist()
    count = len(devices)
    spots = [getattr(d, "coords", None) for d in devices]
    if any(spot is None for spot in spots):
        return count
    row = 1
    while row < count and spots[row][2] == spots[0][2]:
        row += 1
    return row if count % row == 0 else count


def solution(mesh):
    return jax.shard_map(
        functools.partial(body, row_length(mesh)),
        mesh=mesh,
        in_specs=(
            P("member", "region"),
            P("member", "region"),
            P("member", "region"),
            P("region"),
            P("region", None),
            P("region", None, None),
            P("region", None, None),
            P("region", None, None),
        ),
        out_specs=P("member", "region"),
        check_vma=False,
    )
```

profile of v0, /device:TPU:0, one launch (start us, length us, event | category | flops | bytes accessed | tf_op | source)
XLA Modules:
  0.0 446.6 jit_solution(8898684186288799154)
XLA Ops:
  0.0 6.6 %state_pack.1 = (f32[1024,512]{1,0:T(8,128)}, f32[1024,512]{1,0:T(8,128)}) custom-call(f32[128,8192]{1,0:T(8,128)} %in_ref.1), custom_call_target="tpu_custom_call" | custom-call | tf_op jit(solution)/shard_map/state_pack/pallas_call | solution.py:109
  6.6 7.3 %all-to-all-start = ((f32[8,128,512]{2,1,0:T(8,128)}), f32[8,128,512]{2,1,0:T(8,128)S(1)}, u32[]{:S(2)}, u32[]{:S(2)}) async-start(f32[8,128,512]{2,1,0:T(8,128)} %bitcast.114), calls=%async_computation | async-start | bytes 4194304 | tf_op jit(solution)/shard_map/all_to_all | solution.py:93
  13.9 3.4 halo_pack.1
  17.3 1.7 collective-permute-start.1
  20.3 1.7 collective-permute-start.3
  23.1 6.8 %collective-permute-done.2 = f32[4,128]{1,0:T(4,128)S(1)} collective-permute-done((f32[4,128]{1,0:T(4,128)S(1)}, f32[4,128]{1,0:T(4,128)S(1)}, u32[]{:S(2)}, u32[]{:S(2)}) %collective-permute-start.2) | collective-permute-done | bytes 2080 | tf_op jit(solution)/shard_map/ppermute | solution.py:21
  33.1 4.0 window_pack.2
  37.1 4.0 window_pack.3
  41.1 21.0 %all-to-all-done = f32[8,128,512]{2,1,0:T(8,128)S(1)} async-done(((f32[8,128,512]{2,1,0:T(8,128)}), f32[8,128,512]{2,1,0:T(8,128)S(1)}, u32[]{:S(2)}, u32[]{:S(2)}) %all-to-all-start) | async-done | bytes 2097184 | tf_op jit(solution)/shard_map/all_to_all | solution.py:93
  62.1 1.9 copy.21
  64.0 52.0 %all_to_all.70 = f32[8,128,512]{2,1,0:T(8,128)S(1)} all-to-all(f32[8,128,512]{2,1,0:T(8,128)} %bitcast.108), channel_id=1, replica_groups=mesh['member'=8,'region'=4] {'member'}, dimensions={0} | all-to-all | bytes 4194304 | tf_op jit(solution)/shard_map/all_to_all | solution.py:93
  116.0 4.5 %all-to-all-start.2 = ((f32[8,128,512]{2,1,0:T(8,128)}), f32[8,128,512]{2,1,0:T(8,128)}, u32[]{:S(2)}, u32[]{:S(2)}) async-start(f32[8,128,512]{2,1,0:T(8,128)} %bitcast.113), calls=%async_computation.2 | async-start | bytes 4194304 | tf_op jit(solution)/shard_map/all_to_all | solution.py:93
  120.8 2.7 slice.192
  125.0 1.8 reduce_sum.46
  127.0 3.6 fusion.35
  131.2 18.0 %factor_block.4 = f32[128,128]{1,0:T(8,128)} custom-call(f32[128,128]{1,0:T(8,128)} %slice.210.block_ref), custom_call_target="tpu_custom_call" | custom-call | tf_op jit(solution)/shard_map/factor_block/pallas_call | solution.py:206
  150.4 1.7 convolution_subtract_fusion.1
  152.7 18.3 %factor_block.5 = f32[128,128]{1,0:T(8,128)} custom-call(f32[128,128]{1,0:T(8,128)} %slice.213.block_ref), custom_call_target="tpu_custom_call" | custom-call | tf_op jit(solution)/shard_map/factor_block/pallas_call | solution.py:206
  173.3 2.9 copy.22
  176.1 8.3 %all-to-all-start.3 = ((f32[8,128,512]{2,1,0:T(8,128)}), f32[8,128,512]{2,1,0:T(8,128)}, u32[]{:S(2)}, u32[]{:S(2)}) async-start(f32[8,128,512]{2,1,0:T(8,128)} %bitcast.107), calls=%async_computation.3 | async-start | bytes 4194304 | tf_op jit(solution)/shard_map/all_to_all | solution.py:93
  185.8 3.5 fusion.43
  190.8 2.7 slice.197
  193.6 9.9 %collective-permute-start.6 = (f32[1024,384]{0,1:T(8,128)}, f32[1024,384]{0,1:T(8,128)}, u32[]{:S(2)}, u32[]{:S(2)}) collective-permute-start(f32[1024,384]{0,1:T(8,128)} %slice.197), channel_id=1, source_target_pairs={{0,4},{4,12},{12,8},{8,16},{16,20},{20,28},{28,24},{1,5},{5,13},{1... | collective-permute-start | bytes 4718600 | tf_op jit(solution)/shard_map/ppermute | solution.py:313
  203.6 3.8 fusion.53
  207.4 1.8 reduce_sum.47
  210.7 17.9 %factor_block.6 = f32[128,128]{1,0:T(8,128)} custom-call(f32[128,128]{1,0:T(8,128)} %slice.180.block_ref), custom_call_target="tpu_custom_call" | custom-call | tf_op jit(solution)/shard_map/factor_block/pallas_call | solution.py:206
  229.7 1.7 convolution_subtract_fusion.6.block_ref
  231.5 18.0 %factor_block.7 = f32[128,128]{1,0:T(8,128)} custom-call(f32[128,128]{1,0:T(8,128)} %convolution_subtract_fusion.6.block_ref), custom_call_target="tpu_custom_call" | custom-call | tf_op jit(solution)/shard_map/factor_block/pallas_call | solution.py:206
  250.3 4.4 fusion.38
  256.4 4.0 fusion.63
  260.4 1.6 fusion.87
  262.0 2.8 slice_subtract_fusion
  270.5 1.8 convolution_subtract_fusion.2
  273.0 3.0 fusion.68
  276.6 2.7 fusion.105
  279.3 2.7 collective-permute-start.5
  281.9 1.9 fusion.107
  283.8 2.7 fusion.104
  287.9 1.9 fusion.106
  293.6 34.4 %all-to-all-start.4 = ((f32[8,128,256]{2,1,0:T(8,128)}), f32[8,128,256]{2,1,0:T(8,128)}, u32[]{:S(2)}, u32[]{:S(2)}) async-start(f32[8,128,256]{2,1,0:T(8,128)} %bitcast.17), calls=%async_computation.4 | async-start | bytes 2097152 | tf_op jit(solution)/shard_map/all_to_all | solution.py:93
  330.1 2.3 fusion.13
  332.4 23.6 %collective-permute-done.7 = f32[1024,384]{0,1:T(8,128)} collective-permute-done((f32[1024,384]{0,1:T(8,128)}, f32[1024,384]{0,1:T(8,128)}, u32[]{:S(2)}, u32[]{:S(2)}) %collective-permute-start.7) | collective-permute-done | bytes 1572896 | tf_op jit(solution)/shard_map/ppermute | solution.py:336
  356.1 1.7 fusion.12
  357.8 1.9 pad_maximum_fusion
  359.7 2.4 copy.24
  362.1 9.2 %all-to-all-done.4 = f32[8,128,256]{2,1,0:T(8,128)} async-done(((f32[8,128,256]{2,1,0:T(8,128)}), f32[8,128,256]{2,1,0:T(8,128)}, u32[]{:S(2)}, u32[]{:S(2)}) %all-to-all-start.4) | async-done | bytes 1048608 | tf_op jit(solution)/shard_map/all_to_all | solution.py:93
  371.2 68.5 %all_to_all.71 = f32[8,128,768]{2,1,0:T(8,128)} all-to-all(f32[8,128,768]{2,1,0:T(8,128)S(1)} %bitcast.104), channel_id=1, replica_groups=mesh['member'=8,'region'=4] {'member'}, dimensions={0} | all-to-all | bytes 6291456 | tf_op jit(solution)/shard_map/all_to_all | solution.py:93
  439.7 6.6 %state_join.1 = f32[128,8192]{1,0:T(8,128)} custom-call(f32[1024,256]{1,0:T(8,128)} %bitcast.18.centre_ref, f32[1024,768]{1,0:T(8,128)} %bitcast.105), custom_call_target="tpu_custom_call" | custom-call | tf_op jit(solution)/shard_map/state_join/pallas_call | solution.py:136
  (121 shorter events, 34.2 us)
Async XLA Ops:
  6.6 55.5 %all-to-all-start = ((f32[8,128,512]{2,1,0:T(8,128)}), f32[8,128,512]{2,1,0:T(8,128)S(1)}, u32[]{:S(2)}, u32[]{:S(2)}) async-start(f32[8,128,512]{2,1,0:T(8,128)} %bitcast.114), calls=%async_computation | async-start | bytes 4194304 | tf_op jit(solution)/shard_map/all_to_all | solution.py:93
  13.9 5.1 %copy-start.17 = (s32[1,2,4]{2,1,0:T(2,128)S(1)}, s32[1,2,4]{2,1,0:T(2,128)}, u32[]{:S(2)}) copy-start(s32[1,2,4]{2,1,0:T(2,128)} %param.16) | copy-start | bytes 100
  13.9 5.2 %copy-start.16 = (f32[4096]{0:T(1024)S(1)}, f32[4096]{0:T(1024)}, u32[]{:S(2)}) copy-start(f32[4096]{0:T(1024)} %param.13) | copy-start | bytes 49156
  13.9 8.2 %copy-start.15 = (s32[1,8,4]{1,2,0:T(4,128)S(1)}, s32[1,8,4]{1,2,0:T(4,128)}, u32[]{:S(2)}) copy-start(s32[1,8,4]{1,2,0:T(4,128)} %param.15) | copy-start | bytes 388
  17.3 14.2 %collective-permute-start = (f32[128,1024]{1,0:T(8,128)}, f32[128,1024]{1,0:T(8,128)S(1)}, u32[]{:S(2)}, u32[]{:S(2)}) collective-permute-start(f32[128,1024]{1,0:T(8,128)} %get-tuple-element.23), channel_id=1, source_target_pairs={{0,1},{1,2},{2,3},{3,0},{4,5},{5,6},{6,7},{7,4},{8,9},{9,10},{10,1... | collective-permute-start | bytes 1572872 | tf_op jit(solution)/shard_map/ppermute | solution.py:21
  17.3 14.2 %collective-permute-start.1 = (f32[128,1024]{1,0:T(8,128)}, f32[128,1024]{1,0:T(8,128)S(1)}, u32[]{:S(2)}, u32[]{:S(2)}) collective-permute-start(f32[128,1024]{1,0:T(8,128)} %get-tuple-element.24), channel_id=1, source_target_pairs={{0,3},{1,0},{2,1},{3,2},{4,7},{5,4},{6,5},{7,6},{8,11},{9,8},{10,9... | collective-permute-start | bytes 1572872 | tf_op jit(solution)/shard_map/ppermute | solution.py:21
  19.7 10.2 %collective-permute-start.2 = (f32[4,128]{1,0:T(4,128)S(1)}, f32[4,128]{1,0:T(4,128)S(1)}, u32[]{:S(2)}, u32[]{:S(2)}) collective-permute-start(f32[4,128]{1,0:T(4,128)S(1)} %broadcast_select_fusion.1), channel_id=1, source_target_pairs={{0,1},{1,2},{2,3},{3,0},{4,5},{5,6},{6,7},{7,4},{8,9},{9,10},{10,1... | collective-permute-start | bytes 6152 | tf_op jit(solution)/shard_map/ppermute | solution.py:21
  20.3 10.5 %collective-permute-start.3 = (f32[4,128]{1,0:T(4,128)S(1)}, f32[4,128]{1,0:T(4,128)S(1)}, u32[]{:S(2)}, u32[]{:S(2)}) collective-permute-start(f32[4,128]{1,0:T(4,128)S(1)} %broadcast_select_fusion), channel_id=1, source_target_pairs={{0,3},{1,0},{2,1},{3,2},{4,7},{5,4},{6,5},{7,6},{8,11},{9,8},{10,9... | collective-permute-start | bytes 6152 | tf_op jit(solution)/shard_map/ppermute | solution.py:21
  31.5 0.8 copy-start.6
  32.3 0.8 copy-start.7
  116.0 4.5 %copy-start.18 = (s32[1,64,4]{1,2,0:T(4,128)S(1)}, s32[1,64,4]{1,2,0:T(4,128)}, u32[]{:S(2)}) copy-start(s32[1,64,4]{1,2,0:T(4,128)} %param.17) | copy-start | bytes 3076
  116.0 57.3 %all-to-all-start.2 = ((f32[8,128,512]{2,1,0:T(8,128)}), f32[8,128,512]{2,1,0:T(8,128)}, u32[]{:S(2)}, u32[]{:S(2)}) async-start(f32[8,128,512]{2,1,0:T(8,128)} %bitcast.113), calls=%async_computation.2 | async-start | bytes 4194304 | tf_op jit(solution)/shard_map/all_to_all | solution.py:93
  123.5 65.8 %collective-permute-start.4 = (f32[1024,384]{0,1:T(8,128)}, f32[1024,384]{0,1:T(8,128)}, u32[]{:S(2)}, u32[]{:S(2)}) collective-permute-start(f32[1024,384]{0,1:T(8,128)} %slice.192), channel_id=1, source_target_pairs={{4,0},{12,4},{8,12},{16,8},{20,16},{28,20},{24,28},{5,1},{13,5},{9... | collective-permute-start | bytes 4718600 | tf_op jit(solution)/shard_map/ppermute | solution.py:298
  130.5 18.7 %copy-start.13 = (f32[512,512]{1,0:T(8,128)}, f32[512,512]{1,0:T(8,128)S(1)}, u32[]{:S(2)}) copy-start(f32[512,512]{1,0:T(8,128)S(1)} %fusion.35) | copy-start | bytes 3145732
  176.1 84.2 %all-to-all-start.3 = ((f32[8,128,512]{2,1,0:T(8,128)}), f32[8,128,512]{2,1,0:T(8,128)}, u32[]{:S(2)}, u32[]{:S(2)}) async-start(f32[8,128,512]{2,1,0:T(8,128)} %bitcast.107), calls=%async_computation.3 | async-start | bytes 4194304 | tf_op jit(solution)/shard_map/all_to_all | solution.py:93
  193.6 61.1 %collective-permute-start.6 = (f32[1024,384]{0,1:T(8,128)}, f32[1024,384]{0,1:T(8,128)}, u32[]{:S(2)}, u32[]{:S(2)}) collective-permute-start(f32[1024,384]{0,1:T(8,128)} %slice.197), channel_id=1, source_target_pairs={{0,4},{4,12},{12,8},{8,16},{16,20},{20,28},{28,24},{1,5},{5,13},{1... | collective-permute-start | bytes 4718600 | tf_op jit(solution)/shard_map/ppermute | solution.py:313
  262.0 2.9 copy-start.9
  264.9 1.6 copy-start.10
  265.5 2.2 copy-start.14
  272.4 3.6 copy-start.8
  273.0 3.6 copy-start.11
  279.3 4.5 %copy-start.12 = (f32[384,512]{1,0:T(8,128)S(1)}, f32[384,512]{1,0:T(8,128)}, u32[]{:S(2)}) copy-start(f32[384,512]{1,0:T(8,128)} %fusion.63) | copy-start | bytes 2359300
  279.3 50.8 %collective-permute-start.5 = (f32[1024,384]{0,1:T(8,128)}, f32[1024,384]{0,1:T(8,128)}, u32[]{:S(2)}, u32[]{:S(2)}) collective-permute-start(f32[1024,384]{0,1:T(8,128)} %fusion.105), channel_id=1, source_target_pairs={{0,4},{4,12},{12,8},{8,16},{16,20},{20,28},{28,24},{1,5},{5,13},{1... | collective-permute-start | bytes 4718600 | tf_op jit(solution)/shard_map/ppermute | solution.py:337
  283.8 4.0 copy-start.2
  283.8 4.0 copy-start
  283.8 4.1 copy-start.5
  286.5 69.6 %collective-permute-start.7 = (f32[1024,384]{0,1:T(8,128)}, f32[1024,384]{0,1:T(8,128)}, u32[]{:S(2)}, u32[]{:S(2)}) collective-permute-start(f32[1024,384]{0,1:T(8,128)} %fusion.104), channel_id=1, source_target_pairs={{4,0},{12,4},{8,12},{16,8},{20,16},{28,20},{24,28},{5,1},{13,5},{9... | collective-permute-start | bytes 4718600 | tf_op jit(solution)/shard_map/ppermute | solution.py:336
  289.8 1.3 copy-start.3
  292.3 35.7 %copy-start.19 = (s32[1,9]{1,0:T(1,128)S(1)}, s32[1,9]{1,0:T(1,128)}, u32[]{:S(2)}) copy-start(s32[1,9]{1,0:T(1,128)} %param.14) | copy-start | bytes 112
  293.6 77.6 %all-to-all-start.4 = ((f32[8,128,256]{2,1,0:T(8,128)}), f32[8,128,256]{2,1,0:T(8,128)}, u32[]{:S(2)}, u32[]{:S(2)}) async-start(f32[8,128,256]{2,1,0:T(8,128)} %bitcast.17), calls=%async_computation.4 | async-start | bytes 2097152 | tf_op jit(solution)/shard_map/all_to_all | solution.py:93
  330.1 26.0 %copy-start.1 = (f32[1024,512]{0,1:T(8,128)S(1)}, f32[1024,512]{0,1:T(8,128)}, u32[]{:S(2)}) copy-start(f32[1024,512]{0,1:T(8,128)} %copy.22) | copy-start | bytes 6291460
  330.1 26.0 %copy-start.4 = (f32[1024,512]{0,1:T(8,128)S(1)}, f32[1024,512]{0,1:T(8,128)}, u32[]{:S(2)}) copy-start(f32[1024,512]{0,1:T(8,128)} %copy-done.3) | copy-start | bytes 6291460
where the time goes:
time: 451 us; the launch traced here: 447 us
  blocking collectives  120 us (27%)
  Pallas kernels  96.8 us (21%)
  starting transfers between devices  73.2 us (16%)
  waiting for transfers between devices  61.6 us (14%)
  matrix products  52.3 us (12%)
  local copies, waits for them, and re-layouts  25.5 us (6%)
  other arithmetic  15.7 us (3%)
    all_to_all x2, blocking collectives, to_owners(): lax.all_to_all(rows_by_owner, 'member', split_axis=0, concat_axis=0, tile...  120 us
    pallas_call x4, Pallas kernels, factor_block(): pl.pallas_call(factor_kernel, out_shape=jax.ShapeDtypeStruct((size, size)...  72.2 us
    all_to_all x4, starting transfers between devices, to_owners(): lax.all_to_all(rows_by_owner, 'member', split_axis=0, concat_axis=0, tile...  54.4 us
    all_to_all x4, waiting for transfers between devices, to_owners(): lax.all_to_all(rows_by_owner, 'member', split_axis=0, concat_axis=0, tile...  30.2 us
    dot_general x17, matrix products, times_transposed(): lax.dot_general(left, right, (((1,), (1,)), ((), ())), precision=precisio...  24.8 us
    ppermute x1, waiting for transfers between devices, body(): inc_high = lax.ppermute(times_transposed(weights, low_gain), 'member', down)  23.6 us
    dot_general x4, matrix products, masked_gain(): lax.dot_general(centred, perturbed, (((0,), (0,)), ((), ())), precision=h...  15.8 us
    ppermute x1, starting transfers between devices, body(): lax.ppermute(second_states[:, own_width - half - edge:], 'member', up)  9.91 us
  transfers between devices with their start and end apart: 12, of which 5 were waited for; matrix products, arithmetic and copies ran while one was open for 16% of the time, Pallas kernels for 19%

commit v1 on v0

v1 whole, which is shorter than its diff:
```python
import functools

import jax
import jax.numpy as jnp
from jax import lax
from jax.experimental import pallas as pl
from jax.experimental.pallas import tpu as pltpu
from jax.sharding import PartitionSpec as P

PIECE = 128
OBS_PER = 4
LOCAL = OBS_PER * PIECE
TILE = 256

MESH = pl.DeviceIdType.MESH
highest = lax.Precision.HIGHEST


def cols(start, count=1):
    return pl.ds(pl.multiple_of(start * PIECE, PIECE), count * PIECE)


def dot(left, right, contract, precision=None):
    return lax.dot_general(
        left,
        right,
        ((contract[0], contract[1]), ((), ())),
        precision=precision,
        preferred_element_type=jnp.float32,
    )


def at_least(value, bound):
    return jnp.clip(value - bound + 1, 0, 1).astype(jnp.float32)


PLAIN = ((1,), (0,))
BY_ROWS = ((1,), (1,))


def split(value):
    top = value.astype(jnp.bfloat16)
    return top, (value - top.astype(jnp.float32)).astype(jnp.bfloat16)


def factor_block(block, work_ref):
    size = block.shape[0]
    wide = 2 * size
    eye = lax.broadcasted_iota(jnp.int32, (size, size), 0) == lax.broadcasted_iota(
        jnp.int32, (size, size), 1
    )
    work_ref[:, :size] = block
    work_ref[:, size:] = eye.astype(jnp.float32)
    step_rows = 8
    row_ids = lax.broadcasted_iota(jnp.int32, (step_rows, wide), 0)
    for start in range(0, size, step_rows):
        rows = work_ref[start : start + step_rows, :]
        for j in range(step_rows):
            column = rows[:, start + j : start + j + 1]
            scale = 1.0 / jnp.sqrt(column[j : j + 1, :])
            pivot = rows[j : j + 1, :] * scale
            lowered = rows - (column * scale) * pivot
            rows = jnp.where(row_ids > j, lowered, jnp.where(row_ids == j, pivot, rows))
        work_ref[start : start + step_rows, :] = rows
        after = start + step_rows
        if after < size:
            change = dot(rows[:, :size], rows, ((0,), (0,)), highest)
            work_ref[after:, :] = work_ref[after:, :] - change[after:, :]


def snake(index, row, flip):
    return index + (index // row + flip) % 2 * (row - 1 - 2 * (index % row))


def analysis_kernel(
    plan,
    lists_ref,
    ids_ref,
    offsets_ref,
    cover_ref,
    background,
    expected_hbm,
    innov_hbm,
    own_var,
    out,
    expected,
    innov,
    own_e,
    own_d,
    ext_e,
    ext_d,
    ext_var,
    halo_send,
    var_send,
    pack,
    obs,
    devs,
    states,
    turned,
    turned_top,
    turned_low,
    trailing,
    work,
    inverses,
    panels,
    weight_top,
    weight_low,
    gain_top,
    gain_low,
    state_top,
    state_low,
    result,
    edge_inc,
    edge_got,
    member_send,
    member_recv,
    pair_send,
    pair_recv,
    halo_send_sem,
    halo_recv_sem,
    local_sem,
):
    groups, regions, row, per_device, spread = plan
    rows = expected.shape[0]
    own_count = expected.shape[1] // PIECE
    side = ids_ref.shape[1]
    members = groups * rows
    edge = spread * PIECE
    own_width = per_device * PIECE
    middle = own_width - 2 * edge
    me = lax.axis_index("member")
    region = lax.axis_index("region")
    flip = region % 2
    patch = snake(me, row, flip)
    has_dn = patch > 0
    has_up = patch < groups - 1
    member_dn = snake((patch + groups - 1) % groups, row, flip)
    member_up = snake((patch + 1) % groups, row, flip)
    region_after = (region + 1) % regions
    region_before = (region + regions - 1) % regions
    my_rows = pl.ds(pl.multiple_of(me * rows, rows), rows)

    def rows_of(member):
        return pl.ds(pl.multiple_of(member * rows, rows), rows)

    load_e = pltpu.make_async_copy(expected_hbm, expected, local_sem.at[0])
    load_d = pltpu.make_async_copy(innov_hbm, innov, local_sem.at[1])
    load_e.start()
    load_d.start()

    barrier = pltpu.get_barrier_semaphore()
    for k in range(1, groups):
        pl.semaphore_signal(
            barrier, inc=1, device_id=((me + k) % groups, region), device_id_type=MESH
        )
    for other in (region_after, region_before):
        pl.semaphore_signal(barrier, inc=1, device_id=(me, other), device_id_type=MESH)
    pl.semaphore_wait(barrier, groups + 1)

    def state_copy(slot, start, width, k):
        target = (me + k) % groups
        source = snake(target, row, flip) * own_width + start
        return pltpu.make_async_remote_copy(
            src_ref=background.at[:, pl.ds(pl.multiple_of(source, PIECE), width)],
            dst_ref=states.at[my_rows, edge + start : edge + start + width],
            send_sem=member_send.at[slot, k],
            recv_sem=member_recv.at[slot, k],
            device_id=(target, region),
            device_id_type=MESH,
        )

    def state_own(slot, start, width):
        source = patch * own_width + start
        return pltpu.make_async_copy(
            background.at[:, pl.ds(pl.multiple_of(source, PIECE), width)],
            states.at[my_rows, edge + start : edge + start + width],
            member_recv.at[slot, 0],
        )

    def send_states(slot, start, width):
        @pl.loop(1, groups)
        def _(k):
            state_copy(slot, start, width, k).start()

        state_own(slot, start, width).start()

    def take_states(slot, start, width):
        @pl.loop(1, groups)
        def _(k):
            state_copy(slot, start, width, k).wait_recv()

        state_own(slot, start, width).wait()

    def window_copy(slot, source, target_ref, k):
        return pltpu.make_async_remote_copy(
            src_ref=source.at[rows_of((me + k) % groups), :],
            dst_ref=target_ref.at[my_rows, :],
            send_sem=member_send.at[slot, k],
            recv_sem=member_recv.at[slot, k],
            device_id=((me + k) % groups, region),
            device_id_type=MESH,
        )

    def return_copy(slot, start, width, k):
        return pltpu.make_async_remote_copy(
            src_ref=result.at[rows_of((me + k) % groups), start : start + width],
            dst_ref=out.at[
                :, pl.ds(pl.multiple_of(patch * own_width + start, PIECE), width)
            ],
            send_sem=member_send.at[slot, k],
            recv_sem=member_recv.at[slot, k],
            device_id=((me + k) % groups, region),
            device_id_type=MESH,
        )

    def return_own(slot, start, width):
        return pltpu.make_async_copy(
            result.at[my_rows, start : start + width],
            out.at[:, pl.ds(pl.multiple_of(patch * own_width + start, PIECE), width)],
            member_recv.at[slot, 0],
        )

    def send_back(slot, start, width):
        @pl.loop(1, groups)
        def _(k):
            return_copy(slot, start, width, k).start()

        return_own(slot, start, width).start()

    S_MID, S_LOW, S_HIGH, W_E, W_D, R_MID, R_LOW, R_HIGH = range(8)
    pieces_of = {
        S_MID: (edge, middle),
        S_LOW: (0, edge),
        S_HIGH: (own_width - edge, edge),
    }

    for load, flat, own, ext in (
        (load_e, expected, own_e, ext_e),
        (load_d, innov, own_d, ext_d),
    ):
        load.wait()
        for n in range(own_count):
            block = flat[:, n * PIECE : (n + 1) * PIECE]
            own[n] = block
            ext[n] = block
    for n in range(own_count):
        ext_var[n] = own_var[n]
    halo_copies = []
    for part, (own, ext, send) in enumerate(
        ((own_e, ext_e, halo_send.at[0]), (own_var, ext_var, var_send), (own_d, ext_d, halo_send.at[1]))
    ):
        for way, other in ((0, region_after), (1, region_before)):
            for k in range(side):
                send[way, k] = own[ids_ref[way, k]]
            landing = own_count + way * side
            copy = pltpu.make_async_remote_copy(
                src_ref=send.at[way],
                dst_ref=ext.at[landing : landing + side],
                send_sem=halo_send_sem.at[part, way],
                recv_sem=halo_recv_sem.at[part, way],
                device_id=(me, other),
                device_id_type=MESH,
            )
            copy.start()
            halo_copies.append(copy)
    send_states(S_MID, *pieces_of[S_MID])

    def pack_window(ext, buffer, k):
        target = (me + k) % groups
        p = snake(target, row, flip)
        for n in range(OBS_PER):
            buffer[rows_of(target), n * PIECE : (n + 1) * PIECE] = ext[lists_ref[p, n]]

    for copy in halo_copies[:2]:
        copy.wait_recv()

    @pl.loop(1, groups)
    def _(k):
        pack_window(ext_e, pack.at[0], k)
        window_copy(W_E, pack.at[0], obs, k).start()

    pack_window(ext_e, obs, 0)
    for copy in halo_copies[2:]:
        copy.wait_recv()
    variances = [ext_var[lists_ref[patch, n]] for n in range(OBS_PER)]

    @pl.loop(1, groups)
    def _(k):
        pack_window(ext_d, pack.at[1], k)

    pack_window(ext_d, devs, 0)

    @pl.loop(1, groups)
    def _(k):
        window_copy(W_E, pack.at[0], obs, k).wait_send()
        window_copy(W_D, pack.at[1], devs, k).start()

    @pl.loop(1, groups)
    def _(k):
        window_copy(W_E, pack.at[0], obs, k).wait_recv()

    tiles = members // PIECE

    def add_rows(t, total):
        part = obs[pl.ds(pl.multiple_of(t * PIECE, PIECE), PIECE), :]
        return total + jnp.sum(part, axis=0, keepdims=True)

    mean = lax.fori_loop(0, tiles, add_rows, jnp.zeros((1, LOCAL), jnp.float32)) / members

    @pl.loop(0, tiles)
    def _(t):
        place = pl.ds(pl.multiple_of(t * PIECE, PIECE), PIECE)
        part = obs[place, :] - mean
        obs[place, :] = part
        flat = part.T
        turned[:, place] = flat
        top, low = split(flat)
        turned_top[:, place] = top
        turned_low[:, place] = low

    @pl.loop(0, LOCAL // TILE)
    def _(i):
        place = pl.ds(pl.multiple_of(i * TILE, TILE), TILE)

        @pl.loop(0, LOCAL // TILE)
        def _(j):
            other = pl.ds(pl.multiple_of(j * TILE, TILE), TILE)
            trailing[place, other] = dot(
                turned[place, :], obs[:, other], PLAIN, highest
            ) / (members - 1.0)

    eye = lax.broadcasted_iota(jnp.int32, (PIECE, PIECE), 0) == lax.broadcasted_iota(
        jnp.int32, (PIECE, PIECE), 1
    )
    for n in range(OBS_PER):
        place = slice(n * PIECE, (n + 1) * PIECE)
        trailing[place, place] = trailing[place, place] + jnp.where(eye, variances[n], 0.0)

    line = lax.broadcasted_iota(jnp.int32, (LOCAL, PIECE), 0)

    @pl.loop(0, OBS_PER)
    def _(k):
        place = cols(k)
        factor_block(trailing[place, place], work)

        @pl.when(k == 0)
        def _():
            send_states(S_LOW, *pieces_of[S_LOW])

        @pl.when(k == 2)
        def _():
            send_states(S_HIGH, *pieces_of[S_HIGH])

        inverse = work[:, PIECE:]
        inverses[place, :] = inverse
        panel = dot(trailing[:, place], inverse, BY_ROWS, highest)
        panel = jnp.where(line >= (k + 1) * PIECE, panel, 0.0)
        panels[:, place] = panel

        @pl.loop(0, LOCAL // PIECE)
        def _(i):
            part = cols(i)
            trailing[part, :] = trailing[part, :] - dot(
                panels[part, place], panels[:, place], BY_ROWS, highest
            )

    def forward(way):
        start, other = ((edge, member_dn), (own_width, member_up))[way]
        landing = (edge + own_width, 0)[way]
        return pltpu.make_async_remote_copy(
            src_ref=states.at[:, start : start + edge],
            dst_ref=states.at[:, landing : landing + edge],
            send_sem=pair_send.at[way],
            recv_sem=pair_recv.at[way],
            device_id=(other, region),
            device_id_type=MESH,
        )

    def backward(way):
        other = (member_up, member_dn)[way]
        return pltpu.make_async_remote_copy(
            src_ref=edge_inc.at[way],
            dst_ref=edge_got.at[way],
            send_sem=pair_send.at[2 + way],
            recv_sem=pair_recv.at[2 + way],
            device_id=(other, region),
            device_id_type=MESH,
        )

    take_states(S_LOW, *pieces_of[S_LOW])

    @pl.when(has_dn)
    def _():
        forward(0).start()

    @pl.loop(1, groups)
    def _(k):
        window_copy(W_D, pack.at[1], devs, k).wait_recv()

    @pl.loop(0, members // TILE)
    def _(t):
        place = pl.ds(pl.multiple_of(t * TILE, TILE), TILE)
        rest = devs[place, :]
        parts = []
        for k in range(OBS_PER):
            at = slice(k * PIECE, (k + 1) * PIECE)
            part = dot(rest[:, :PIECE], inverses[at, :], BY_ROWS, highest)
            parts.append(part)
            if k + 1 < OBS_PER:
                rest = rest[:, PIECE:] - dot(
                    part, panels[(k + 1) * PIECE :, at], BY_ROWS, highest
                )
        done = None
        for k in reversed(range(OBS_PER)):
            at = slice(k * PIECE, (k + 1) * PIECE)
            part = parts[k]
            if done is not None:
                part = part - dot(done, panels[(k + 1) * PIECE :, at], PLAIN, highest)
            part = dot(part, inverses[at, :], PLAIN, highest)
            done = part if done is None else jnp.concatenate([part, done], axis=1)
        top, low = split(done)
        weight_top[place, :] = top
        weight_low[place, :] = low

    blocks_total = cover_ref.shape[0]

    def find_gain(start, width):
        def add_states(t, total):
            part = states[
                pl.ds(pl.multiple_of(t * PIECE, PIECE), PIECE), start : start + width
            ]
            return total + jnp.sum(part, axis=0, keepdims=True)

        centre = (
            lax.fori_loop(0, tiles, add_states, jnp.zeros((1, width), jnp.float32))
            / members
        )

        @pl.loop(0, tiles)
        def _(t):
            place = pl.ds(pl.multiple_of(t * PIECE, PIECE), PIECE)
            top, low = split(states[place, start : start + width] - centre)
            state_top[place, :width] = top
            state_low[place, :width] = low

        first = patch * per_device - spread + start // PIECE

        @pl.loop(0, OBS_PER)
        def _(n):
            place = cols(n)
            left_top, left_low = turned_top[place, :], turned_low[place, :]
            right_top, right_low = state_top[:, :width], state_low[:, :width]
            gain = (
                dot(left_top, right_top, PLAIN)
                + dot(left_top, right_low, PLAIN)
                + dot(left_low, right_top, PLAIN)
            ) / (members - 1.0)
            for b in range(width // PIECE):
                at = slice(b * PIECE, (b + 1) * PIECE)
                spot = jnp.clip(first + b, 0, blocks_total - 1)
                top, low = split(gain[:, at] * cover_ref[spot, n].astype(jnp.float32))
                gain_top[place, at] = top
                gain_low[place, at] = low

    def increments(width, store):
        @pl.loop(0, members // TILE)
        def _(t):
            place = pl.ds(pl.multiple_of(t * TILE, TILE), TILE)
            left_top, left_low = weight_top[place, :], weight_low[place, :]
            right_top, right_low = gain_top[:, :width], gain_low[:, :width]
            store(
                place,
                dot(left_top, right_top, PLAIN)
                + dot(left_top, right_low, PLAIN)
                + dot(left_low, right_top, PLAIN),
            )

    def own_part(start, width):
        def store(place, value):
            result[place, start : start + width] = (
                states[place, edge + start : edge + start + width] + value
            )

        find_gain(edge + start, width)
        increments(width, store)

    def other_part(way):
        def store(place, value):
            edge_inc[way, place, :] = value

        find_gain((edge + own_width, 0)[way], edge)
        increments(edge, store)
        backward(way).start()

    def settle(way):
        start = (0, own_width - edge)[way]
        bound = offsets_ref[patch + way] - patch * per_device

        @pl.loop(0, members // TILE)
        def _(t):
            place = pl.ds(pl.multiple_of(t * TILE, TILE), TILE)
            for b in range(spread):
                block = start // PIECE + b
                foreign = at_least(bound, block + 1) if way == 0 else at_least(block, bound)
                at = slice(start + b * PIECE, start + (b + 1) * PIECE)
                theirs = (
                    states[place, edge + start + b * PIECE : edge + start + (b + 1) * PIECE]
                    + edge_got[way, place, b * PIECE : (b + 1) * PIECE]
                )
                result[place, at] = theirs * foreign + result[place, at] * (1.0 - foreign)

    take_states(S_MID, *pieces_of[S_MID])
    own_part(edge, middle)
    send_back(R_MID, edge, middle)
    take_states(S_HIGH, *pieces_of[S_HIGH])

    @pl.when(has_up)
    def _():
        forward(1).start()

    own_part(0, edge)

    @pl.when(has_up)
    def _():
        forward(0).wait_recv()
        other_part(0)

    own_part(own_width - edge, edge)

    @pl.when(has_dn)
    def _():
        forward(1).wait_recv()
        other_part(1)
        backward(0).wait_recv()
        settle(0)

    send_back(R_LOW, 0, edge)

    @pl.when(has_up)
    def _():
        backward(1).wait_recv()
        settle(1)

    send_back(R_HIGH, own_width - edge, edge)

    for copy in halo_copies:
        copy.wait_send()

    @pl.when(has_dn)
    def _():
        forward(0).wait_send()
        backward(1).wait_send()

    @pl.when(has_up)
    def _():
        forward(1).wait_send()
        backward(0).wait_send()

    for slot, (start, width) in pieces_of.items():

        @pl.loop(1, groups)
        def _(k):
            state_copy(slot, start, width, k).wait_send()

    @pl.loop(1, groups)
    def _(k):
        window_copy(W_D, pack.at[1], devs, k).wait_send()

    for slot, (start, width) in (
        (R_MID, pieces_of[S_MID]),
        (R_LOW, pieces_of[S_LOW]),
        (R_HIGH, pieces_of[S_HIGH]),
    ):

        @pl.loop(1, groups)
        def _(k):
            return_copy(slot, start, width, k).wait()

        return_own(slot, start, width).wait()


def body(
    row,
    background_realizations,
    realization_expected_data,
    departure_values,
    instrument_dispersion,
    window_piece_offsets,
    window_data_pieces,
    neighbor_piece_ids,
    coupling_indicator,
):
    groups = lax.axis_size("member")
    regions = lax.axis_size("region")
    rows, variable_total = background_realizations.shape
    obs_width = realization_expected_data.shape[1]
    members = groups * rows
    per_device = variable_total // PIECE // groups
    spread = (per_device - 1) // 2
    own_width = per_device * PIECE
    edge = spread * PIECE
    widest = max(edge, own_width - 2 * edge)
    side = neighbor_piece_ids.shape[-1]
    own_count = obs_width // PIECE
    ext_count = own_count + 2 * side
    f32, bf16 = jnp.float32, jnp.bfloat16
    smem = pl.BlockSpec(memory_space=pltpu.SMEM)
    hbm = pl.BlockSpec(memory_space=pl.ANY)
    return pl.pallas_call(
        functools.partial(analysis_kernel, (groups, regions, row, per_device, spread)),
        out_shape=jax.ShapeDtypeStruct((rows, variable_total), f32),
        in_specs=[smem, smem, smem, smem, hbm, hbm, hbm, pl.BlockSpec(memory_space=pltpu.VMEM)],
        out_specs=hbm,
        scratch_shapes=[
            pltpu.VMEM((rows, obs_width), f32),
            pltpu.VMEM((rows, obs_width), f32),
            pltpu.VMEM((own_count, rows, PIECE), f32),
            pltpu.VMEM((own_count, rows, PIECE), f32),
            pltpu.VMEM((ext_count, rows, PIECE), f32),
            pltpu.VMEM((ext_count, rows, PIECE), f32),
            pltpu.VMEM((ext_count, 1, PIECE), f32),
            pltpu.VMEM((2, 2, side, rows, PIECE), f32),
            pltpu.VMEM((2, side, 1, PIECE), f32),
            pltpu.VMEM((2, members, LOCAL), f32),
            pltpu.VMEM((members, LOCAL), f32),
            pltpu.VMEM((members, LOCAL), f32),
            pltpu.VMEM((members, own_width + 2 * edge), f32),
            pltpu.VMEM((LOCAL, members), f32),
            pltpu.VMEM((LOCAL, members), bf16),
            pltpu.VMEM((LOCAL, members), bf16),
            pltpu.VMEM((LOCAL, LOCAL), f32),
            pltpu.VMEM((PIECE, 2 * PIECE), f32),
            pltpu.VMEM((LOCAL, PIECE), f32),
            pltpu.VMEM((LOCAL, LOCAL), f32),
            pltpu.VMEM((members, LOCAL), bf16),
            pltpu.VMEM((members, LOCAL), bf16),
            pltpu.VMEM((LOCAL, widest), bf16),
            pltpu.VMEM((LOCAL, widest), bf16),
            pltpu.VMEM((members, widest), bf16),
            pltpu.VMEM((members, widest), bf16),
            pltpu.VMEM((members, own_width), f32),
            pltpu.VMEM((2, members, edge), f32),
            pltpu.VMEM((2, members, edge), f32),
            pltpu.SemaphoreType.DMA((8, groups)),
            pltpu.SemaphoreType.DMA((8, groups)),
            pltpu.SemaphoreType.DMA((4,)),
            pltpu.SemaphoreType.DMA((4,)),
            pltpu.SemaphoreType.DMA((3, 2)),
            pltpu.SemaphoreType.DMA((3, 2)),
            pltpu.SemaphoreType.DMA((2,)),
        ],
        compiler_params=pltpu.CompilerParams(
            collective_id=0, has_side_effects=True, vmem_limit_bytes=60 * 1024 * 1024
        ),
        name="analysis",
    )(
        window_data_pieces[0],
        neighbor_piece_ids[0],
        window_piece_offsets[0],
        coupling_indicator[0],
        background_realizations,
        realization_expected_data,
        departure_values,
        instrument_dispersion.reshape(-1, 1, PIECE),
    )


def row_length(mesh):
    devices = mesh.devices[:, 0].tolist()
    count = len(devices)
    spots = [getattr(d, "coords", None) for d in devices]
    if any(spot is None for spot in spots):
        return count
    row = 1
    while row < count and spots[row][2] == spots[0][2]:
        row += 1
    return row if count % row == 0 else count


def solution(mesh):
    return jax.shard_map(
        functools.partial(body, row_length(mesh)),
        mesh=mesh,
        in_specs=(
            P("member", "region"),
            P("member", "region"),
            P("member", "region"),
            P("region"),
            P("region", None),
            P("region", None, None),
            P("region", None, None),
            P("region", None, None),
        ),
        out_specs=P("member", "region"),
        check_vma=False,
    )
```

time: 451 us -> 349 us (0.77)
  the two profiles are of different devices: /device:TPU:0 before, /device:TPU:13 now
where the time goes in v1:
time: 349 us; the launch traced here: 348 us
  Pallas kernels  341 us (98%)
  local copies, waits for them, and re-layouts  7.34 us (2%)
    pallas_call x1, Pallas kernels, body(): pl.pallas_call(functools.partial(analysis_kernel, (groups, regions, row,...  341 us

profile of v1, /device:TPU:13, one launch (start us, length us, event | category | flops | bytes accessed | tf_op | source)
XLA Modules:
  0.0 348.2 jit_solution(6939957910720217776)
XLA Ops:
  0.0 1.3 copy.10.lists_ref
  1.4 1.4 copy.9
  2.7 340.9 %analysis.1 = f32[128,8192]{1,0:T(8,128)} custom-call(s32[8,4]{1,0:T(8,128)} %copy.10.lists_ref, s32[2,4]{1,0:T(2,128)} %bitcast.8, s32[9]{0:T(128)} %bitcast.9, s32[64,4]{1,0:T(8,128)} %bitcast.5, f32[128,8192]{1,0:T(8,128)} %background.1, f32[128,4096]{1,0:T(8,128)} %expected_hbm.1, f32[128,4096]{1,0:T(8,128)} %innov_hbm.1, f32[32,1,128]{2,1,0:T(1,128)} %bitcast.6), custom_call_target="tpu_custom_call" | custom-call | tf_op jit(solution)/shard_map/analysis/pallas_call | solution.py:609
  343.6 4.6 %copy.12 = f32[128,8192]{1,0:T(8,128)} copy(f32[128,8192]{1,0:T(8,128)} %analysis.1) | data formatting | bytes 8388608

commit v2 on v1

--- a/solution.py
+++ b/solution.py
@@ -81,7 +81,7 @@
     background,
     expected_hbm,
     innov_hbm,
-    own_var,
+    flat_var,
     out,
     expected,
     innov,
@@ -89,6 +89,7 @@
     own_d,
     ext_e,
     ext_d,
+    own_var,
     ext_var,
     halo_send,
     var_send,
@@ -112,6 +113,7 @@
     result,
     edge_inc,
     edge_got,
+    cross_got,
     member_send,
     member_recv,
     pair_send,
@@ -123,7 +125,7 @@
     groups, regions, row, per_device, spread = plan
     rows = expected.shape[0]
     own_count = expected.shape[1] // PIECE
-    side = ids_ref.shape[1]
+    side = ids_ref.shape[2]
     members = groups * rows
     edge = spread * PIECE
     own_width = per_device * PIECE
@@ -134,6 +136,14 @@
     patch = snake(me, row, flip)
     has_dn = patch > 0
     has_up = patch < groups - 1
+    near, far = groups // 2 - 1, groups // 2
+    is_near, is_far = patch == near, patch == far
+    gives_dn = jnp.logical_and(has_dn, patch != far)
+    gives_up = jnp.logical_and(has_up, patch != near)
+    owner_near = snake(near, row, flip)
+    owner_far = snake(far, row, flip)
+    lower = groups // 2
+    in_lower = me < lower
     member_dn = snake((patch + groups - 1) % groups, row, flip)
     member_up = snake((patch + 1) % groups, row, flip)
     region_after = (region + 1) % regions
@@ -191,6 +201,53 @@
 
         state_own(slot, start, width).wait()
 
+    def middle_place(way):
+        start = (near * own_width + own_width - edge, far * own_width)[way]
+        landing = (0, edge + own_width)[way]
+        return (
+            background.at[:, start : start + edge],
+            states.at[my_rows, landing : landing + edge],
+        )
+
+    def middle_copy(way, sender):
+        source, target = middle_place(way)
+        return pltpu.make_async_remote_copy(
+            src_ref=source,
+            dst_ref=target,
+            send_sem=member_send.at[S_X, way],
+            recv_sem=member_recv.at[S_X, sender],
+            device_id=((owner_far, owner_near)[way], region),
+            device_id_type=MESH,
+        )
+
+    def middle_own(way):
+        return pltpu.make_async_copy(*middle_place(way), local_sem.at[2])
+
+    def send_middle():
+        for way, mine in ((0, is_far), (1, is_near)):
+
+            @pl.when(jnp.logical_not(mine))
+            def _():
+                middle_copy(way, me).start()
+
+            @pl.when(mine)
+            def _():
+                middle_own(way).start()
+
+    def sent_middle():
+        for way, mine in ((0, is_far), (1, is_near)):
+
+            @pl.when(jnp.logical_not(mine))
+            def _():
+                middle_copy(way, me).wait_send()
+
+    def take_middle(way):
+        @pl.loop(1, groups)
+        def _(k):
+            middle_copy(way, (me + groups - k) % groups).wait_recv()
+
+        middle_own(way).wait()
+
     def window_copy(slot, source, target_ref, k):
         return pltpu.make_async_remote_copy(
             src_ref=source.at[rows_of((me + k) % groups), :],
@@ -220,19 +277,103 @@
             member_recv.at[slot, 0],
         )
 
+    def returns(slot, p, member):
+        if slot == R_LOW:
+            return jnp.logical_or(p != far, member >= lower)
+        if slot == R_HIGH:
+            return jnp.logical_or(p != near, member < lower)
+        return p >= 0
+
     def send_back(slot, start, width):
         @pl.loop(1, groups)
         def _(k):
-            return_copy(slot, start, width, k).start()
-
-        return_own(slot, start, width).start()
-
-    S_MID, S_LOW, S_HIGH, W_E, W_D, R_MID, R_LOW, R_HIGH = range(8)
+            @pl.when(returns(slot, patch, (me + k) % groups))
+            def _():
+                return_copy(slot, start, width, k).start()
+
+        @pl.when(returns(slot, patch, me))
+        def _():
+            return_own(slot, start, width).start()
+
+    def end_back(slot, start, width):
+        @pl.loop(1, groups)
+        def _(k):
+            @pl.when(returns(slot, patch, (me + k) % groups))
+            def _():
+                return_copy(slot, start, width, k).wait_send()
+
+            @pl.when(returns(slot, snake((me + groups - k) % groups, row, flip), me))
+            def _():
+                return_copy(slot, start, width, k).wait_recv()
+
+        @pl.when(returns(slot, patch, me))
+        def _():
+            return_own(slot, start, width).wait()
+
+    def cross_place(way, member):
+        start = (far * own_width, near * own_width + own_width - edge)[way]
+        return (
+            edge_inc.at[way, rows_of(member), :],
+            out.at[:, start : start + edge],
+        )
+
+    def cross_copy(way, member):
+        source, target = cross_place(way, member)
+        return pltpu.make_async_remote_copy(
+            src_ref=source,
+            dst_ref=target,
+            send_sem=member_send.at[R_X, member],
+            recv_sem=member_recv.at[R_X, 0],
+            device_id=(member, region),
+            device_id_type=MESH,
+        )
+
+    def cross_own(way):
+        return pltpu.make_async_copy(*cross_place(way, me), local_sem.at[3])
+
+    crossing = ((0, is_near, owner_near, 0, lower), (1, is_far, owner_far, lower, groups))
+
+    def send_cross(way):
+        first, last = crossing[way][3:]
+
+        @pl.loop(first, last)
+        def _(member):
+            @pl.when(member != me)
+            def _():
+                cross_copy(way, member).start()
+
+        @pl.when(jnp.logical_and(me >= first, me < last))
+        def _():
+            cross_own(way).start()
+
+    def end_cross():
+        for way, mine, owner, first, last in crossing:
+            inside = jnp.logical_and(me >= first, me < last)
+
+            @pl.when(mine)
+            def _():
+                @pl.loop(first, last)
+                def _(member):
+                    @pl.when(member != me)
+                    def _():
+                        cross_copy(way, member).wait_send()
+
+                @pl.when(inside)
+                def _():
+                    cross_own(way).wait()
+
+            @pl.when(jnp.logical_and(inside, me != owner))
+            def _():
+                cross_copy(way, me).wait_recv()
+
+    S_MID, S_LOW, S_HIGH, W_E, W_D, R_MID, R_LOW, R_HIGH, S_X, R_X = range(10)
     pieces_of = {
         S_MID: (edge, middle),
         S_LOW: (0, edge),
         S_HIGH: (own_width - edge, edge),
     }
+
+    send_states(S_MID, *pieces_of[S_MID])
 
     for load, flat, own, ext in (
         (load_e, expected, own_e, ext_e),
@@ -244,14 +385,15 @@
             own[n] = block
             ext[n] = block
     for n in range(own_count):
-        ext_var[n] = own_var[n]
+        own_var[n] = flat_var[n : n + 1, :]
+        ext_var[n] = flat_var[n : n + 1, :]
     halo_copies = []
     for part, (own, ext, send) in enumerate(
         ((own_e, ext_e, halo_send.at[0]), (own_var, ext_var, var_send), (own_d, ext_d, halo_send.at[1]))
     ):
         for way, other in ((0, region_after), (1, region_before)):
             for k in range(side):
-                send[way, k] = own[ids_ref[way, k]]
+                send[way, k] = own[ids_ref[0, way, k]]
             landing = own_count + way * side
             copy = pltpu.make_async_remote_copy(
                 src_ref=send.at[way],
@@ -263,13 +405,12 @@
             )
             copy.start()
             halo_copies.append(copy)
-    send_states(S_MID, *pieces_of[S_MID])
 
     def pack_window(ext, buffer, k):
         target = (me + k) % groups
         p = snake(target, row, flip)
         for n in range(OBS_PER):
-            buffer[rows_of(target), n * PIECE : (n + 1) * PIECE] = ext[lists_ref[p, n]]
+            buffer[rows_of(target), n * PIECE : (n + 1) * PIECE] = ext[lists_ref[0, p, n]]
 
     for copy in halo_copies[:2]:
         copy.wait_recv()
@@ -282,7 +423,7 @@
     pack_window(ext_e, obs, 0)
     for copy in halo_copies[2:]:
         copy.wait_recv()
-    variances = [ext_var[lists_ref[patch, n]] for n in range(OBS_PER)]
+    variances = [ext_var[lists_ref[0, patch, n]] for n in range(OBS_PER)]
 
     @pl.loop(1, groups)
     def _(k):
@@ -349,6 +490,7 @@
 
         @pl.when(k == 2)
         def _():
+            send_middle()
             send_states(S_HIGH, *pieces_of[S_HIGH])
 
         inverse = work[:, PIECE:]
@@ -389,7 +531,7 @@
 
     take_states(S_LOW, *pieces_of[S_LOW])
 
-    @pl.when(has_dn)
+    @pl.when(gives_dn)
     def _():
         forward(0).start()
 
@@ -422,7 +564,7 @@
         weight_top[place, :] = top
         weight_low[place, :] = low
 
-    blocks_total = cover_ref.shape[0]
+    blocks_total = cover_ref.shape[1]
 
     def find_gain(start, width):
         def add_states(t, total):
@@ -458,7 +600,7 @@
             for b in range(width // PIECE):
                 at = slice(b * PIECE, (b + 1) * PIECE)
                 spot = jnp.clip(first + b, 0, blocks_total - 1)
-                top, low = split(gain[:, at] * cover_ref[spot, n].astype(jnp.float32))
+                top, low = split(gain[:, at] * cover_ref[0, spot, n].astype(jnp.float32))
                 gain_top[place, at] = top
                 gain_low[place, at] = low
 
@@ -485,76 +627,182 @@
         increments(width, store)
 
     def other_part(way):
+        place_in = (edge + own_width, 0)[way]
+
         def store(place, value):
-            edge_inc[way, place, :] = value
-
-        find_gain((edge + own_width, 0)[way], edge)
+            edge_inc[way, place, :] = states[place, place_in : place_in + edge] + value
+
+        find_gain(place_in, edge)
         increments(edge, store)
-        backward(way).start()
-
-    def settle(way):
+
+    def foreign(way, owner, b):
         start = (0, own_width - edge)[way]
-        bound = offsets_ref[patch + way] - patch * per_device
-
-        @pl.loop(0, members // TILE)
+        bound = offsets_ref[0, owner + way] - owner * per_device
+        block = start // PIECE + b
+        return at_least(bound, block + 1) if way == 0 else at_least(block, bound)
+
+    half_rows = lower * rows
+
+    def settle(way, first=0, last=members):
+        start = (0, own_width - edge)[way]
+
+        @pl.loop(first // PIECE, last // PIECE)
         def _(t):
-            place = pl.ds(pl.multiple_of(t * TILE, TILE), TILE)
+            place = pl.ds(pl.multiple_of(t * PIECE, PIECE), PIECE)
             for b in range(spread):
-                block = start // PIECE + b
-                foreign = at_least(bound, block + 1) if way == 0 else at_least(block, bound)
+                share = foreign(way, patch, b)
                 at = slice(start + b * PIECE, start + (b + 1) * PIECE)
-                theirs = (
-                    states[place, edge + start + b * PIECE : edge + start + (b + 1) * PIECE]
-                    + edge_got[way, place, b * PIECE : (b + 1) * PIECE]
-                )
-                result[place, at] = theirs * foreign + result[place, at] * (1.0 - foreign)
+                theirs = edge_got[way, place, b * PIECE : (b + 1) * PIECE]
+                result[place, at] = theirs * share + result[place, at] * (1.0 - share)
+
+    def settle_cross(way, owner, first, last):
+        @pl.loop(first // PIECE, last // PIECE)
+        def _(t):
+            place = pl.ds(pl.multiple_of(t * PIECE, PIECE), PIECE)
+            for b in range(spread):
+                share = foreign(way, owner, b)
+                at = slice(b * PIECE, (b + 1) * PIECE)
+                mine = edge_inc[way, place, at]
+                theirs = cross_got[place, at]
+                edge_inc[way, place, at] = mine * share + theirs * (1.0 - share)
+
+    def swap(near_sends, part):
+        first = half_rows if near_sends else 0
+        count = members - half_rows if near_sends else half_rows
+        sent = slice(first, first + count)
+        if part == 0:
+            way = 0 if near_sends else 1
+            source = edge_inc.at[way, sent, :]
+            target = edge_got.at[way, sent, :]
+        else:
+            start = own_width - edge if near_sends else 0
+            source = result.at[sent, start : start + edge]
+            target = cross_got.at[sent, :]
+        return pltpu.make_async_remote_copy(
+            src_ref=source,
+            dst_ref=target,
+            send_sem=pair_send.at[4 + part],
+            recv_sem=pair_recv.at[4 + part],
+            device_id=(owner_far if near_sends else owner_near, region),
+            device_id_type=MESH,
+        )
 
     take_states(S_MID, *pieces_of[S_MID])
     own_part(edge, middle)
     send_back(R_MID, edge, middle)
     take_states(S_HIGH, *pieces_of[S_HIGH])
 
+    @pl.when(gives_up)
+    def _():
+        forward(1).start()
+
+    @pl.when(is_far)
+    def _():
+        take_middle(0)
+
+    @pl.when(is_near)
+    def _():
+        take_middle(1)
+
+    own_part(0, edge)
+
+    @pl.when(is_far)
+    def _():
+        swap(False, 1).start()
+
     @pl.when(has_up)
     def _():
-        forward(1).start()
-
-    own_part(0, edge)
-
-    @pl.when(has_up)
-    def _():
-        forward(0).wait_recv()
+        @pl.when(gives_up)
+        def _():
+            forward(0).wait_recv()
+
         other_part(0)
 
+        @pl.when(gives_up)
+        def _():
+            backward(0).start()
+
+        @pl.when(is_near)
+        def _():
+            swap(True, 0).start()
+
     own_part(own_width - edge, edge)
 
+    @pl.when(is_near)
+    def _():
+        swap(True, 1).start()
+
     @pl.when(has_dn)
     def _():
-        forward(1).wait_recv()
+        @pl.when(gives_dn)
+        def _():
+            forward(1).wait_recv()
+
         other_part(1)
-        backward(0).wait_recv()
-        settle(0)
+
+        @pl.when(gives_dn)
+        def _():
+            backward(1).start()
+            backward(0).wait_recv()
+            settle(0)
+
+        @pl.when(is_far)
+        def _():
+            swap(False, 0).start()
+            swap(True, 0).wait_recv()
+            settle(0, half_rows, members)
 
     send_back(R_LOW, 0, edge)
 
-    @pl.when(has_up)
+    @pl.when(gives_up)
     def _():
         backward(1).wait_recv()
         settle(1)
 
+    @pl.when(is_near)
+    def _():
+        swap(False, 0).wait_recv()
+        settle(1, 0, half_rows)
+
     send_back(R_HIGH, own_width - edge, edge)
+
+    @pl.when(is_near)
+    def _():
+        swap(True, 0).wait_send()
+        swap(False, 1).wait_recv()
+        settle_cross(0, far, 0, half_rows)
+        send_cross(0)
+
+    @pl.when(is_far)
+    def _():
+        swap(False, 0).wait_send()
+        swap(True, 1).wait_recv()
+        settle_cross(1, near, half_rows, members)
+        send_cross(1)
 
     for copy in halo_copies:
         copy.wait_send()
 
-    @pl.when(has_dn)
+    @pl.when(gives_dn)
     def _():
         forward(0).wait_send()
         backward(1).wait_send()
 
-    @pl.when(has_up)
+    @pl.when(gives_up)
     def _():
         forward(1).wait_send()
         backward(0).wait_send()
+
+    @pl.when(is_near)
+    def _():
+        swap(True, 1).wait_send()
+
+    @pl.when(is_far)
+    def _():
+        swap(False, 1).wait_send()
+
+    sent_middle()
+    end_cross()
 
     for slot, (start, width) in pieces_of.items():
 
@@ -571,12 +819,7 @@
         (R_LOW, pieces_of[S_LOW]),
         (R_HIGH, pieces_of[S_HIGH]),
     ):
-
-        @pl.loop(1, groups)
-        def _(k):
-            return_copy(slot, start, width, k).wait()
-
-        return_own(slot, start, width).wait()
+        end_back(slot, start, width)
 
 
 def body(
@@ -618,6 +861,7 @@
             pltpu.VMEM((own_count, rows, PIECE), f32),
             pltpu.VMEM((ext_count, rows, PIECE), f32),
             pltpu.VMEM((ext_count, rows, PIECE), f32),
+            pltpu.VMEM((own_count, 1, PIECE), f32),
             pltpu.VMEM((ext_count, 1, PIECE), f32),
             pltpu.VMEM((2, 2, side, rows, PIECE), f32),
             pltpu.VMEM((2, side, 1, PIECE), f32),
@@ -641,27 +885,28 @@
             pltpu.VMEM((members, own_width), f32),
             pltpu.VMEM((2, members, edge), f32),
             pltpu.VMEM((2, members, edge), f32),
-            pltpu.SemaphoreType.DMA((8, groups)),
-            pltpu.SemaphoreType.DMA((8, groups)),
-            pltpu.SemaphoreType.DMA((4,)),
-            pltpu.SemaphoreType.DMA((4,)),
+            pltpu.VMEM((members, edge), f32),
+            pltpu.SemaphoreType.DMA((10, groups)),
+            pltpu.SemaphoreType.DMA((10, groups)),
+            pltpu.SemaphoreType.DMA((6,)),
+            pltpu.SemaphoreType.DMA((6,)),
             pltpu.SemaphoreType.DMA((3, 2)),
             pltpu.SemaphoreType.DMA((3, 2)),
-            pltpu.SemaphoreType.DMA((2,)),
+            pltpu.SemaphoreType.DMA((4,)),
         ],
         compiler_params=pltpu.CompilerParams(
             collective_id=0, has_side_effects=True, vmem_limit_bytes=60 * 1024 * 1024
         ),
         name="analysis",
     )(
-        window_data_pieces[0],
-        neighbor_piece_ids[0],
-        window_piece_offsets[0],
-        coupling_indicator[0],
+        window_data_pieces,
+        neighbor_piece_ids,
+        window_piece_offsets,
+        coupling_indicator,
         background_realizations,
         realization_expected_data,
         departure_values,
-        instrument_dispersion.reshape(-1, 1, PIECE),
+        instrument_dispersion.reshape(-1, PIECE),
     )
 
 

time: 349 us -> 340 us (0.974)
  Pallas kernels: 341 us -> 332 us
    pallas_call x1, Pallas kernels: 341 us -> 332 us  [body(): pl.pallas_call(functools.partial(analysis_kernel, (groups, regions, row,...]
    unnamed x2 -> x3, local copies, waits for them, and re-layouts: 5.99 us -> 7.34 us
where the time goes in v2:
time: 340 us; the launch traced here: 339 us
  Pallas kernels  332 us (98%)
  local copies, waits for them, and re-layouts  7.34 us (2%)
    pallas_call x1, Pallas kernels, body(): pl.pallas_call(functools.partial(analysis_kernel, (groups, regions, row,...  332 us
    unnamed x3, local copies, waits for them, and re-layouts  7.34 us

profile of v2, /device:TPU:13, one launch (start us, length us, event | category | flops | bytes accessed | tf_op | source)
XLA Modules:
  0.0 339.4 jit_solution(6962741968371283131)
XLA Ops:
  0.0 1.3 copy.9.lists_ref
  1.4 1.4 copy.10.cover_ref
  2.7 332.1 %analysis.1 = f32[128,8192]{1,0:T(8,128)} custom-call(s32[1,8,4]{2,1,0:T(8,128)} %copy.9.lists_ref, s32[1,2,4]{2,1,0:T(2,128)} %ids_ref.1, s32[1,9]{1,0:T(1,128)} %offsets_ref.1, s32[1,64,4]{2,1,0:T(8,128)} %copy.10.cover_ref, f32[128,8192]{1,0:T(8,128)} %background.1, f32[128,4096]{1,0:T(8,128)} %expected_hbm.1, f32[128,4096]{1,0:T(8,128)} %innov_hbm.1, ...), custom_call_target="tpu_custom_call" | custom-call | tf_op jit(solution)/shard_map/analysis/pallas_call | solution.py:852
  334.8 4.6 %copy.12 = f32[128,8192]{1,0:T(8,128)} copy(f32[128,8192]{1,0:T(8,128)} %analysis.1) | data formatting | bytes 8388608

commit v3 on v2

--- a/solution.py
+++ b/solution.py
@@ -366,9 +366,10 @@
             def _():
                 cross_copy(way, me).wait_recv()
 
-    S_MID, S_LOW, S_HIGH, W_E, W_D, R_MID, R_LOW, R_HIGH, S_X, R_X = range(10)
+    S_MID, S_NEXT, S_LOW, S_HIGH, W_E, W_D, R_MID, R_LOW, R_HIGH, S_X, R_X = range(11)
     pieces_of = {
-        S_MID: (edge, middle),
+        S_MID: (edge, PIECE),
+        S_NEXT: (edge + PIECE, middle - PIECE),
         S_LOW: (0, edge),
         S_HIGH: (own_width - edge, edge),
     }
@@ -410,7 +411,7 @@
         target = (me + k) % groups
         p = snake(target, row, flip)
         for n in range(OBS_PER):
-            buffer[rows_of(target), n * PIECE : (n + 1) * PIECE] = ext[lists_ref[0, p, n]]
+            buffer[rows_of(target), n * PIECE : (n + 1) * PIECE] = ext[lists_ref[0, n, p]]
 
     for copy in halo_copies[:2]:
         copy.wait_recv()
@@ -423,7 +424,7 @@
     pack_window(ext_e, obs, 0)
     for copy in halo_copies[2:]:
         copy.wait_recv()
-    variances = [ext_var[lists_ref[0, patch, n]] for n in range(OBS_PER)]
+    variances = [ext_var[lists_ref[0, n, patch]] for n in range(OBS_PER)]
 
     @pl.loop(1, groups)
     def _(k):
@@ -434,7 +435,10 @@
     @pl.loop(1, groups)
     def _(k):
         window_copy(W_E, pack.at[0], obs, k).wait_send()
-        window_copy(W_D, pack.at[1], devs, k).start()
+
+    send_states(S_LOW, *pieces_of[S_LOW])
+    send_middle()
+    send_states(S_HIGH, *pieces_of[S_HIGH])
 
     @pl.loop(1, groups)
     def _(k):
@@ -477,35 +481,6 @@
         place = slice(n * PIECE, (n + 1) * PIECE)
         trailing[place, place] = trailing[place, place] + jnp.where(eye, variances[n], 0.0)
 
-    line = lax.broadcasted_iota(jnp.int32, (LOCAL, PIECE), 0)
-
-    @pl.loop(0, OBS_PER)
-    def _(k):
-        place = cols(k)
-        factor_block(trailing[place, place], work)
-
-        @pl.when(k == 0)
-        def _():
-            send_states(S_LOW, *pieces_of[S_LOW])
-
-        @pl.when(k == 2)
-        def _():
-            send_middle()
-            send_states(S_HIGH, *pieces_of[S_HIGH])
-
-        inverse = work[:, PIECE:]
-        inverses[place, :] = inverse
-        panel = dot(trailing[:, place], inverse, BY_ROWS, highest)
-        panel = jnp.where(line >= (k + 1) * PIECE, panel, 0.0)
-        panels[:, place] = panel
-
-        @pl.loop(0, LOCAL // PIECE)
-        def _(i):
-            part = cols(i)
-            trailing[part, :] = trailing[part, :] - dot(
-                panels[part, place], panels[:, place], BY_ROWS, highest
-            )
-
     def forward(way):
         start, other = ((edge, member_dn), (own_width, member_up))[way]
         landing = (edge + own_width, 0)[way]
@@ -529,11 +504,90 @@
             device_id_type=MESH,
         )
 
-    take_states(S_LOW, *pieces_of[S_LOW])
-
-    @pl.when(gives_dn)
-    def _():
-        forward(0).start()
+    line = lax.broadcasted_iota(jnp.int32, (LOCAL, PIECE), 0)
+
+    @pl.loop(0, OBS_PER)
+    def _(k):
+        place = cols(k)
+        @pl.when(k == 2)
+        def _():
+            @pl.loop(1, groups)
+            def _(j):
+                window_copy(W_D, pack.at[1], devs, j).start()
+
+            send_states(S_NEXT, *pieces_of[S_NEXT])
+
+        @pl.when(k == 3)
+        def _():
+            take_states(S_LOW, *pieces_of[S_LOW])
+
+            @pl.when(gives_dn)
+            def _():
+                forward(0).start()
+
+            take_states(S_HIGH, *pieces_of[S_HIGH])
+
+            @pl.when(gives_up)
+            def _():
+                forward(1).start()
+
+        factor_block(trailing[place, place], work)
+
+        inverse = work[:, PIECE:]
+        inverses[place, :] = inverse
+        panel = dot(trailing[:, place], inverse, BY_ROWS, highest)
+        panel = jnp.where(line >= (k + 1) * PIECE, panel, 0.0)
+        panels[:, place] = panel
+
+        @pl.loop(0, LOCAL // PIECE)
+        def _(i):
+            part = cols(i)
+            trailing[part, :] = trailing[part, :] - dot(
+                panels[part, place], panels[:, place], BY_ROWS, highest
+            )
+
+    blocks_total = cover_ref.shape[2]
+
+    def find_gain(start, width):
+        def add_states(t, total):
+            part = states[
+                pl.ds(pl.multiple_of(t * PIECE, PIECE), PIECE), start : start + width
+            ]
+            return total + jnp.sum(part, axis=0, keepdims=True)
+
+        centre = (
+            lax.fori_loop(0, tiles, add_states, jnp.zeros((1, width), jnp.float32))
+            / members
+        )
+
+        @pl.loop(0, tiles)
+        def _(t):
+            place = pl.ds(pl.multiple_of(t * PIECE, PIECE), PIECE)
+            top, low = split(states[place, start : start + width] - centre)
+            state_top[place, :width] = top
+            state_low[place, :width] = low
+
+        first = patch * per_device - spread + start // PIECE
+
+        @pl.loop(0, OBS_PER)
+        def _(n):
+            place = cols(n)
+            left_top, left_low = turned_top[place, :], turned_low[place, :]
+            right_top, right_low = state_top[:, :width], state_low[:, :width]
+            gain = (
+                dot(left_top, right_top, PLAIN)
+                + dot(left_top, right_low, PLAIN)
+                + dot(left_low, right_top, PLAIN)
+            ) / (members - 1.0)
+            for b in range(width // PIECE):
+                at = slice(b * PIECE, (b + 1) * PIECE)
+                spot = jnp.clip(first + b, 0, blocks_total - 1)
+                top, low = split(gain[:, at] * cover_ref[0, n, spot].astype(jnp.float32))
+                gain_top[place, start + b * PIECE : start + (b + 1) * PIECE] = top
+                gain_low[place, start + b * PIECE : start + (b + 1) * PIECE] = low
+
+    find_gain(edge, edge)
+    find_gain(own_width, edge)
 
     @pl.loop(1, groups)
     def _(k):
@@ -564,52 +618,13 @@
         weight_top[place, :] = top
         weight_low[place, :] = low
 
-    blocks_total = cover_ref.shape[1]
-
-    def find_gain(start, width):
-        def add_states(t, total):
-            part = states[
-                pl.ds(pl.multiple_of(t * PIECE, PIECE), PIECE), start : start + width
-            ]
-            return total + jnp.sum(part, axis=0, keepdims=True)
-
-        centre = (
-            lax.fori_loop(0, tiles, add_states, jnp.zeros((1, width), jnp.float32))
-            / members
-        )
-
-        @pl.loop(0, tiles)
-        def _(t):
-            place = pl.ds(pl.multiple_of(t * PIECE, PIECE), PIECE)
-            top, low = split(states[place, start : start + width] - centre)
-            state_top[place, :width] = top
-            state_low[place, :width] = low
-
-        first = patch * per_device - spread + start // PIECE
-
-        @pl.loop(0, OBS_PER)
-        def _(n):
-            place = cols(n)
-            left_top, left_low = turned_top[place, :], turned_low[place, :]
-            right_top, right_low = state_top[:, :width], state_low[:, :width]
-            gain = (
-                dot(left_top, right_top, PLAIN)
-                + dot(left_top, right_low, PLAIN)
-                + dot(left_low, right_top, PLAIN)
-            ) / (members - 1.0)
-            for b in range(width // PIECE):
-                at = slice(b * PIECE, (b + 1) * PIECE)
-                spot = jnp.clip(first + b, 0, blocks_total - 1)
-                top, low = split(gain[:, at] * cover_ref[0, spot, n].astype(jnp.float32))
-                gain_top[place, at] = top
-                gain_low[place, at] = low
-
-    def increments(width, store):
+    def increments(start, width, store):
         @pl.loop(0, members // TILE)
         def _(t):
             place = pl.ds(pl.multiple_of(t * TILE, TILE), TILE)
             left_top, left_low = weight_top[place, :], weight_low[place, :]
-            right_top, right_low = gain_top[:, :width], gain_low[:, :width]
+            right_top = gain_top[:, start : start + width]
+            right_low = gain_low[:, start : start + width]
             store(
                 place,
                 dot(left_top, right_top, PLAIN)
@@ -623,8 +638,7 @@
                 states[place, edge + start : edge + start + width] + value
             )
 
-        find_gain(edge + start, width)
-        increments(width, store)
+        increments(edge + start, width, store)
 
     def other_part(way):
         place_in = (edge + own_width, 0)[way]
@@ -633,7 +647,7 @@
             edge_inc[way, place, :] = states[place, place_in : place_in + edge] + value
 
         find_gain(place_in, edge)
-        increments(edge, store)
+        increments(place_in, edge, store)
 
     def foreign(way, owner, b):
         start = (0, own_width - edge)[way]
@@ -687,70 +701,72 @@
             device_id_type=MESH,
         )
 
+    @pl.when(has_up)
+    def _():
+        @pl.when(gives_up)
+        def _():
+            forward(0).wait_recv()
+
+        @pl.when(is_near)
+        def _():
+            take_middle(1)
+
+        other_part(0)
+
+        @pl.when(gives_up)
+        def _():
+            backward(0).start()
+
+        @pl.when(is_near)
+        def _():
+            swap(True, 0).start()
+
+    @pl.when(has_dn)
+    def _():
+        @pl.when(gives_dn)
+        def _():
+            forward(1).wait_recv()
+
+        @pl.when(is_far)
+        def _():
+            take_middle(0)
+
+        other_part(1)
+
+        @pl.when(gives_dn)
+        def _():
+            backward(1).start()
+
+        @pl.when(is_far)
+        def _():
+            swap(False, 0).start()
+
     take_states(S_MID, *pieces_of[S_MID])
+    take_states(S_NEXT, *pieces_of[S_NEXT])
+    find_gain(edge + edge, middle)
     own_part(edge, middle)
     send_back(R_MID, edge, middle)
-    take_states(S_HIGH, *pieces_of[S_HIGH])
-
-    @pl.when(gives_up)
-    def _():
-        forward(1).start()
+    own_part(0, edge)
 
     @pl.when(is_far)
     def _():
-        take_middle(0)
+        swap(False, 1).start()
+
+    own_part(own_width - edge, edge)
 
     @pl.when(is_near)
     def _():
-        take_middle(1)
-
-    own_part(0, edge)
+        swap(True, 1).start()
+
+    @pl.when(gives_dn)
+    def _():
+        backward(0).wait_recv()
+        settle(0)
 
     @pl.when(is_far)
     def _():
-        swap(False, 1).start()
-
-    @pl.when(has_up)
-    def _():
-        @pl.when(gives_up)
-        def _():
-            forward(0).wait_recv()
-
-        other_part(0)
-
-        @pl.when(gives_up)
-        def _():
-            backward(0).start()
-
-        @pl.when(is_near)
-        def _():
-            swap(True, 0).start()
-
-    own_part(own_width - edge, edge)
-
-    @pl.when(is_near)
-    def _():
-        swap(True, 1).start()
-
-    @pl.when(has_dn)
-    def _():
-        @pl.when(gives_dn)
-        def _():
-            forward(1).wait_recv()
-
-        other_part(1)
-
-        @pl.when(gives_dn)
-        def _():
-            backward(1).start()
-            backward(0).wait_recv()
-            settle(0)
-
-        @pl.when(is_far)
-        def _():
-            swap(False, 0).start()
-            swap(True, 0).wait_recv()
-            settle(0, half_rows, members)
+        swap(True, 0).wait_recv()
+        settle(0, half_rows, members)
 
     send_back(R_LOW, 0, edge)
 
@@ -815,7 +831,7 @@
         window_copy(W_D, pack.at[1], devs, k).wait_send()
 
     for slot, (start, width) in (
-        (R_MID, pieces_of[S_MID]),
+        (R_MID, (edge, middle)),
         (R_LOW, pieces_of[S_LOW]),
         (R_HIGH, pieces_of[S_HIGH]),
     ):
@@ -878,16 +894,16 @@
             pltpu.VMEM((LOCAL, LOCAL), f32),
             pltpu.VMEM((members, LOCAL), bf16),
             pltpu.VMEM((members, LOCAL), bf16),
-            pltpu.VMEM((LOCAL, widest), bf16),
-            pltpu.VMEM((LOCAL, widest), bf16),
+            pltpu.VMEM((LOCAL, own_width + 2 * edge), bf16),
+            pltpu.VMEM((LOCAL, own_width + 2 * edge), bf16),
             pltpu.VMEM((members, widest), bf16),
             pltpu.VMEM((members, widest), bf16),
             pltpu.VMEM((members, own_width), f32),
             pltpu.VMEM((2, members, edge), f32),
             pltpu.VMEM((2, members, edge), f32),
             pltpu.VMEM((members, edge), f32),
-            pltpu.SemaphoreType.DMA((10, groups)),
-            pltpu.SemaphoreType.DMA((10, groups)),
+            pltpu.SemaphoreType.DMA((11, groups)),
+            pltpu.SemaphoreType.DMA((11, groups)),
             pltpu.SemaphoreType.DMA((6,)),
             pltpu.SemaphoreType.DMA((6,)),
             pltpu.SemaphoreType.DMA((3, 2)),
@@ -899,10 +915,10 @@
         ),
         name="analysis",
     )(
-        window_data_pieces,
+        window_data_pieces.swapaxes(1, 2),
         neighbor_piece_ids,
         window_piece_offsets,
-        coupling_indicator,
+        coupling_indicator.swapaxes(1, 2),
         background_realizations,
         realization_expected_data,
         departure_values,

time: 340 us -> 322 us (0.947)
  Pallas kernels: 332 us -> 315 us
    pallas_call x1, Pallas kernels: 332 us -> 315 us  [body(): pl.pallas_call(functools.partial(analysis_kernel, (groups, regions, row,...]
    unnamed x3 -> x1, local copies, waits for them, and re-layouts: 7.34 us -> 4.61 us
where the time goes in v3:
time: 322 us; the launch traced here: 319 us
  Pallas kernels  315 us (98%)
  local copies, waits for them, and re-layouts  4.61 us (1%)
    pallas_call x1, Pallas kernels, body(): pl.pallas_call(functools.partial(analysis_kernel, (groups, regions, row,...  315 us

profile of v3, /device:TPU:13, one launch (start us, length us, event | category | flops | bytes accessed | tf_op | source)
XLA Modules:
  0.0 319.3 jit_solution(16439446891834904200)
XLA Ops:
  0.0 314.7 %analysis.1 = f32[128,8192]{1,0:T(8,128)} custom-call(s32[1,4,8]{2,1,0:T(4,128)} %bitcast.4, s32[1,2,4]{2,1,0:T(2,128)} %ids_ref.1, s32[1,9]{1,0:T(1,128)} %offsets_ref.1, s32[1,4,64]{2,1,0:T(4,128)} %bitcast.5, f32[128,8192]{1,0:T(8,128)} %background.1, f32[128,4096]{1,0:T(8,128)} %expected_hbm.1, f32[128,4096]{1,0:T(8,128)} %innov_hbm.1, f32[32,128]{1,0:T(8,128)} %bitcast.3), custom_call_target="tpu_custom_call" | custom-call | tf_op jit(solution)/shard_map/analysis/pallas_call | solution.py:868
  314.7 4.6 %copy.10 = f32[128,8192]{1,0:T(8,128)} copy(f32[128,8192]{1,0:T(8,128)} %analysis.1) | data formatting | bytes 8388608

commit v4 on v3

--- a/solution.py
+++ b/solution.py
@@ -102,7 +102,7 @@
     turned_low,
     trailing,
     work,
-    inverses,
+    lowered,
     panels,
     weight_top,
     weight_low,
@@ -118,6 +118,8 @@
     member_recv,
     pair_send,
     pair_recv,
+    back_send,
+    back_recv,
     halo_send_sem,
     halo_recv_sem,
     local_sem,
@@ -278,9 +280,9 @@
         )
 
     def returns(slot, p, member):
-        if slot == R_LOW:
+        if R_LOW <= slot < R_HIGH:
             return jnp.logical_or(p != far, member >= lower)
-        if slot == R_HIGH:
+        if slot >= R_HIGH:
             return jnp.logical_or(p != near, member < lower)
         return p >= 0
 
@@ -366,7 +368,8 @@
             def _():
                 cross_copy(way, me).wait_recv()
 
-    S_MID, S_NEXT, S_LOW, S_HIGH, W_E, W_D, R_MID, R_LOW, R_HIGH, S_X, R_X = range(11)
+    S_MID, S_NEXT, S_LOW, S_HIGH, W_E, W_D, S_X, R_X, R_MID, R_LOW = range(10)
+    R_HIGH = R_LOW + spread
     pieces_of = {
         S_MID: (edge, PIECE),
         S_NEXT: (edge + PIECE, middle - PIECE),
@@ -493,18 +496,23 @@
             device_id_type=MESH,
         )
 
-    def backward(way):
+    def backward(way, b):
         other = (member_up, member_dn)[way]
+        at = slice(b * PIECE, (b + 1) * PIECE)
         return pltpu.make_async_remote_copy(
-            src_ref=edge_inc.at[way],
-            dst_ref=edge_got.at[way],
-            send_sem=pair_send.at[2 + way],
-            recv_sem=pair_recv.at[2 + way],
+            src_ref=edge_inc.at[way, :, at],
+            dst_ref=edge_got.at[way, :, at],
+            send_sem=back_send.at[way, b],
+            recv_sem=back_recv.at[way, b],
             device_id=(other, region),
             device_id_type=MESH,
         )
 
     line = lax.broadcasted_iota(jnp.int32, (LOCAL, PIECE), 0)
+    for n in range(OBS_PER):
+        place = slice(n * PIECE, (n + 1) * PIECE)
+        lowered[place, :] = jnp.zeros((PIECE, LOCAL), jnp.float32)
+        lowered[place, place] = eye.astype(jnp.float32)
 
     @pl.loop(0, OBS_PER)
     def _(k):
@@ -515,16 +523,14 @@
             def _(j):
                 window_copy(W_D, pack.at[1], devs, j).start()
 
-            send_states(S_NEXT, *pieces_of[S_NEXT])
+            take_states(S_LOW, *pieces_of[S_LOW])
+
+            @pl.when(gives_dn)
+            def _():
+                forward(0).start()
 
         @pl.when(k == 3)
         def _():
-            take_states(S_LOW, *pieces_of[S_LOW])
-
-            @pl.when(gives_dn)
-            def _():
-                forward(0).start()
-
             take_states(S_HIGH, *pieces_of[S_HIGH])
 
             @pl.when(gives_up)
@@ -534,16 +540,19 @@
         factor_block(trailing[place, place], work)
 
         inverse = work[:, PIECE:]
-        inverses[place, :] = inverse
+        lowered[place, :] = dot(inverse, lowered[place, :], PLAIN, highest)
         panel = dot(trailing[:, place], inverse, BY_ROWS, highest)
         panel = jnp.where(line >= (k + 1) * PIECE, panel, 0.0)
-        panels[:, place] = panel
+        panels[...] = panel
 
         @pl.loop(0, LOCAL // PIECE)
         def _(i):
             part = cols(i)
             trailing[part, :] = trailing[part, :] - dot(
-                panels[part, place], panels[:, place], BY_ROWS, highest
+                panels[part, :], panels[...], BY_ROWS, highest
+            )
+            lowered[part, :] = lowered[part, :] - dot(
+                panels[part, :], lowered[place, :], PLAIN, highest
             )
 
     blocks_total = cover_ref.shape[2]
@@ -586,8 +595,30 @@
                 gain_top[place, start + b * PIECE : start + (b + 1) * PIECE] = top
                 gain_low[place, start + b * PIECE : start + (b + 1) * PIECE] = low
 
+    send_states(S_NEXT, *pieces_of[S_NEXT])
+
+    @pl.loop(0, LOCAL // PIECE)
+    def _(i):
+        part = cols(i)
+        trailing[part, :] = dot(lowered[:, part].T, lowered[...], PLAIN, highest)
+
     find_gain(edge, edge)
     find_gain(own_width, edge)
+    take_states(S_MID, *pieces_of[S_MID])
+    find_gain(edge + edge, PIECE)
+
+    @pl.when(has_up)
+    def _():
+        @pl.when(gives_up)
+        def _():
+            forward(0).wait_recv()
+
+        @pl.when(is_near)
+        def _():
+            take_middle(1)
+
+        find_gain(edge + own_width, edge)
+
 
     @pl.loop(1, groups)
     def _(k):
@@ -596,25 +627,7 @@
     @pl.loop(0, members // TILE)
     def _(t):
         place = pl.ds(pl.multiple_of(t * TILE, TILE), TILE)
-        rest = devs[place, :]
-        parts = []
-        for k in range(OBS_PER):
-            at = slice(k * PIECE, (k + 1) * PIECE)
-            part = dot(rest[:, :PIECE], inverses[at, :], BY_ROWS, highest)
-            parts.append(part)
-            if k + 1 < OBS_PER:
-                rest = rest[:, PIECE:] - dot(
-                    part, panels[(k + 1) * PIECE :, at], BY_ROWS, highest
-                )
-        done = None
-        for k in reversed(range(OBS_PER)):
-            at = slice(k * PIECE, (k + 1) * PIECE)
-            part = parts[k]
-            if done is not None:
-                part = part - dot(done, panels[(k + 1) * PIECE :, at], PLAIN, highest)
-            part = dot(part, inverses[at, :], PLAIN, highest)
-            done = part if done is None else jnp.concatenate([part, done], axis=1)
-        top, low = split(done)
+        top, low = split(dot(devs[place, :], trailing[...], PLAIN, highest))
         weight_top[place, :] = top
         weight_low[place, :] = low
 
@@ -646,7 +659,6 @@
         def store(place, value):
             edge_inc[way, place, :] = states[place, place_in : place_in + edge] + value
 
-        find_gain(place_in, edge)
         increments(place_in, edge, store)
 
     def foreign(way, owner, b):
@@ -657,17 +669,16 @@
 
     half_rows = lower * rows
 
-    def settle(way, first=0, last=members):
+    def settle(way, b, first=0, last=members):
         start = (0, own_width - edge)[way]
+        share = foreign(way, patch, b)
+        at = slice(start + b * PIECE, start + (b + 1) * PIECE)
 
         @pl.loop(first // PIECE, last // PIECE)
         def _(t):
             place = pl.ds(pl.multiple_of(t * PIECE, PIECE), PIECE)
-            for b in range(spread):
-                share = foreign(way, patch, b)
-                at = slice(start + b * PIECE, start + (b + 1) * PIECE)
-                theirs = edge_got[way, place, b * PIECE : (b + 1) * PIECE]
-                result[place, at] = theirs * share + result[place, at] * (1.0 - share)
+            theirs = edge_got[way, place, b * PIECE : (b + 1) * PIECE]
+            result[place, at] = theirs * share + result[place, at] * (1.0 - share)
 
     def settle_cross(way, owner, first, last):
         @pl.loop(first // PIECE, last // PIECE)
@@ -703,49 +714,43 @@
 
     @pl.when(has_up)
     def _():
+        other_part(0)
+
         @pl.when(gives_up)
         def _():
-            forward(0).wait_recv()
+            for b in range(spread):
+                backward(0, b).start()
 
         @pl.when(is_near)
         def _():
-            take_middle(1)
-
-        other_part(0)
-
-        @pl.when(gives_up)
-        def _():
-            backward(0).start()
-
-        @pl.when(is_near)
-        def _():
             swap(True, 0).start()
 
-    @pl.when(has_dn)
-    def _():
-        @pl.when(gives_dn)
-        def _():
-            forward(1).wait_recv()
-
-        @pl.when(is_far)
-        def _():
-            take_middle(0)
-
-        other_part(1)
-
-        @pl.when(gives_dn)
-        def _():
-            backward(1).start()
-
-        @pl.when(is_far)
-        def _():
-            swap(False, 0).start()
-
-    take_states(S_MID, *pieces_of[S_MID])
     take_states(S_NEXT, *pieces_of[S_NEXT])
-    find_gain(edge + edge, middle)
+    find_gain(edge + edge + PIECE, middle - PIECE)
     own_part(edge, middle)
     send_back(R_MID, edge, middle)
+    @pl.when(has_dn)
+    def _():
+        @pl.when(gives_dn)
+        def _():
+            forward(1).wait_recv()
+
+        @pl.when(is_far)
+        def _():
+            take_middle(0)
+
+        find_gain(0, edge)
+        other_part(1)
+
+        @pl.when(gives_dn)
+        def _():
+            for b in range(spread):
+                backward(1, b).start()
+
+        @pl.when(is_far)
+        def _():
+            swap(False, 0).start()
+
     own_part(0, edge)
 
     @pl.when(is_far)
@@ -758,29 +763,37 @@
     def _():
         swap(True, 1).start()
 
-    @pl.when(gives_dn)
-    def _():
-        backward(0).wait_recv()
-        settle(0)
-
     @pl.when(is_far)
     def _():
         swap(True, 0).wait_recv()
-        settle(0, half_rows, members)
-
-    send_back(R_LOW, 0, edge)
-
-    @pl.when(gives_up)
-    def _():
-        backward(1).wait_recv()
-        settle(1)
 
     @pl.when(is_near)
     def _():
         swap(False, 0).wait_recv()
-        settle(1, 0, half_rows)
-
-    send_back(R_HIGH, own_width - edge, edge)
+
+    for b in range(spread):
+
+        @pl.when(gives_dn)
+        def _():
+            backward(0, b).wait_recv()
+            settle(0, b)
+
+        @pl.when(is_far)
+        def _():
+            settle(0, b, half_rows, members)
+
+        send_back(R_LOW + b, b * PIECE, PIECE)
+
+        @pl.when(gives_up)
+        def _():
+            backward(1, b).wait_recv()
+            settle(1, b)
+
+        @pl.when(is_near)
+        def _():
+            settle(1, b, 0, half_rows)
+
+        send_back(R_HIGH + b, own_width - edge + b * PIECE, PIECE)
 
     @pl.when(is_near)
     def _():
@@ -802,12 +815,14 @@
     @pl.when(gives_dn)
     def _():
         forward(0).wait_send()
-        backward(1).wait_send()
+        for b in range(spread):
+            backward(1, b).wait_send()
 
     @pl.when(gives_up)
     def _():
         forward(1).wait_send()
-        backward(0).wait_send()
+        for b in range(spread):
+            backward(0, b).wait_send()
 
     @pl.when(is_near)
     def _():
@@ -830,12 +845,10 @@
     def _(k):
         window_copy(W_D, pack.at[1], devs, k).wait_send()
 
-    for slot, (start, width) in (
-        (R_MID, (edge, middle)),
-        (R_LOW, pieces_of[S_LOW]),
-        (R_HIGH, pieces_of[S_HIGH]),
-    ):
-        end_back(slot, start, width)
+    end_back(R_MID, edge, middle)
+    for b in range(spread):
+        end_back(R_LOW + b, b * PIECE, PIECE)
+        end_back(R_HIGH + b, own_width - edge + b * PIECE, PIECE)
 
 
 def body(
@@ -890,8 +903,8 @@
             pltpu.VMEM((LOCAL, members), bf16),
             pltpu.VMEM((LOCAL, LOCAL), f32),
             pltpu.VMEM((PIECE, 2 * PIECE), f32),
+            pltpu.VMEM((LOCAL, LOCAL), f32),
             pltpu.VMEM((LOCAL, PIECE), f32),
-            pltpu.VMEM((LOCAL, LOCAL), f32),
             pltpu.VMEM((members, LOCAL), bf16),
             pltpu.VMEM((members, LOCAL), bf16),
             pltpu.VMEM((LOCAL, own_width + 2 * edge), bf16),
@@ -902,10 +915,12 @@
             pltpu.VMEM((2, members, edge), f32),
             pltpu.VMEM((2, members, edge), f32),
             pltpu.VMEM((members, edge), f32),
-            pltpu.SemaphoreType.DMA((11, groups)),
-            pltpu.SemaphoreType.DMA((11, groups)),
+            pltpu.SemaphoreType.DMA((9 + 2 * spread, groups)),
+            pltpu.SemaphoreType.DMA((9 + 2 * spread, groups)),
             pltpu.SemaphoreType.DMA((6,)),
             pltpu.SemaphoreType.DMA((6,)),
+            pltpu.SemaphoreType.DMA((2, spread)),
+            pltpu.SemaphoreType.DMA((2, spread)),
             pltpu.SemaphoreType.DMA((3, 2)),
             pltpu.SemaphoreType.DMA((3, 2)),
             pltpu.SemaphoreType.DMA((4,)),

time: 322 us -> 308 us (0.957)
  Pallas kernels: 315 us -> 301 us
    pallas_call x1, Pallas kernels: 315 us -> 301 us  [body(): pl.pallas_call(functools.partial(analysis_kernel, (groups, regions, row,...]
where the time goes in v4:
time: 308 us; the launch traced here: 306 us
  Pallas kernels  301 us (98%)
  local copies, waits for them, and re-layouts  4.61 us (1%)
    pallas_call x1, Pallas kernels, body(): pl.pallas_call(functools.partial(analysis_kernel, (groups, regions, row,...  301 us

profile of v4, /device:TPU:13, one launch (start us, length us, event | category | flops | bytes accessed | tf_op | source)
XLA Modules:
  0.0 306.0 jit_solution(6402473094067731541)
XLA Ops:
  0.0 301.4 %analysis.1 = f32[128,8192]{1,0:T(8,128)} custom-call(s32[1,4,8]{2,1,0:T(4,128)} %bitcast.4, s32[1,2,4]{2,1,0:T(2,128)} %ids_ref.1, s32[1,9]{1,0:T(1,128)} %offsets_ref.1, s32[1,4,64]{2,1,0:T(4,128)} %bitcast.5, f32[128,8192]{1,0:T(8,128)} %background.1, f32[128,4096]{1,0:T(8,128)} %expected_hbm.1, f32[128,4096]{1,0:T(8,128)} %innov_hbm.1, f32[32,128]{1,0:T(8,128)} %bitcast.3), custom_call_target="tpu_custom_call" | custom-call | tf_op jit(solution)/shard_map/analysis/pallas_call | solution.py:881
  301.4 4.6 %copy.10 = f32[128,8192]{1,0:T(8,128)} copy(f32[128,8192]{1,0:T(8,128)} %analysis.1) | data formatting | bytes 8388608

commit v5 on v4

--- a/solution.py
+++ b/solution.py
@@ -368,7 +368,7 @@
             def _():
                 cross_copy(way, me).wait_recv()
 
-    S_MID, S_NEXT, S_LOW, S_HIGH, W_E, W_D, S_X, R_X, R_MID, R_LOW = range(10)
+    S_MID, S_NEXT, S_LOW, S_HIGH, W_E, W_D, S_X, R_X, R_MID, R_NEXT, R_LOW = range(11)
     R_HIGH = R_LOW + spread
     pieces_of = {
         S_MID: (edge, PIECE),
@@ -537,6 +537,8 @@
             def _():
                 forward(1).start()
 
+            send_states(S_NEXT, *pieces_of[S_NEXT])
+
         factor_block(trailing[place, place], work)
 
         inverse = work[:, PIECE:]
@@ -594,8 +596,6 @@
                 top, low = split(gain[:, at] * cover_ref[0, n, spot].astype(jnp.float32))
                 gain_top[place, start + b * PIECE : start + (b + 1) * PIECE] = top
                 gain_low[place, start + b * PIECE : start + (b + 1) * PIECE] = low
-
-    send_states(S_NEXT, *pieces_of[S_NEXT])
 
     @pl.loop(0, LOCAL // PIECE)
     def _(i):
@@ -712,6 +712,8 @@
             device_id_type=MESH,
         )
 
+    own_part(edge, PIECE)
+    send_back(R_MID, edge, PIECE)
     @pl.when(has_up)
     def _():
         other_part(0)
@@ -727,8 +729,8 @@
 
     take_states(S_NEXT, *pieces_of[S_NEXT])
     find_gain(edge + edge + PIECE, middle - PIECE)
-    own_part(edge, middle)
-    send_back(R_MID, edge, middle)
+    own_part(edge + PIECE, middle - PIECE)
+    send_back(R_NEXT, edge + PIECE, middle - PIECE)
     @pl.when(has_dn)
     def _():
         @pl.when(gives_dn)
@@ -845,7 +847,8 @@
     def _(k):
         window_copy(W_D, pack.at[1], devs, k).wait_send()
 
-    end_back(R_MID, edge, middle)
+    end_back(R_MID, edge, PIECE)
+    end_back(R_NEXT, edge + PIECE, middle - PIECE)
     for b in range(spread):
         end_back(R_LOW + b, b * PIECE, PIECE)
         end_back(R_HIGH + b, own_width - edge + b * PIECE, PIECE)
@@ -915,8 +918,8 @@
             pltpu.VMEM((2, members, edge), f32),
             pltpu.VMEM((2, members, edge), f32),
             pltpu.VMEM((members, edge), f32),
-            pltpu.SemaphoreType.DMA((9 + 2 * spread, groups)),
-            pltpu.SemaphoreType.DMA((9 + 2 * spread, groups)),
+            pltpu.SemaphoreType.DMA((10 + 2 * spread, groups)),
+            pltpu.SemaphoreType.DMA((10 + 2 * spread, groups)),
             pltpu.SemaphoreType.DMA((6,)),
             pltpu.SemaphoreType.DMA((6,)),
             pltpu.SemaphoreType.DMA((2, spread)),

time: 308 us -> 305 us (level)
  Pallas kernels: 301 us -> 296 us
    pallas_call x1, Pallas kernels: 301 us -> 296 us  [body(): pl.pallas_call(functools.partial(analysis_kernel, (groups, regions, row,...]
where the time goes in v5:
time: 305 us; the launch traced here: 301 us
  Pallas kernels  296 us (97%)
  local copies, waits for them, and re-layouts  4.61 us (2%)
    pallas_call x1, Pallas kernels, body(): pl.pallas_call(functools.partial(analysis_kernel, (groups, regions, row,...  296 us

profile of v5, /device:TPU:13, one launch (start us, length us, event | category | flops | bytes accessed | tf_op | source)
XLA Modules:
  0.0 300.6 jit_solution(5394822152310218067)
XLA Ops:
  0.0 296.0 %analysis.1 = f32[128,8192]{1,0:T(8,128)} custom-call(s32[1,4,8]{2,1,0:T(4,128)} %bitcast.4, s32[1,2,4]{2,1,0:T(2,128)} %ids_ref.1, s32[1,9]{1,0:T(1,128)} %offsets_ref.1, s32[1,4,64]{2,1,0:T(4,128)} %bitcast.5, f32[128,8192]{1,0:T(8,128)} %background.1, f32[128,4096]{1,0:T(8,128)} %expected_hbm.1, f32[128,4096]{1,0:T(8,128)} %innov_hbm.1, f32[32,128]{1,0:T(8,128)} %bitcast.3), custom_call_target="tpu_custom_call" | custom-call | tf_op jit(solution)/shard_map/analysis/pallas_call | solution.py:884
  296.0 4.6 %copy.10 = f32[128,8192]{1,0:T(8,128)} copy(f32[128,8192]{1,0:T(8,128)} %analysis.1) | data formatting | bytes 8388608

commit v6 on v5

--- a/solution.py
+++ b/solution.py
@@ -438,8 +438,9 @@
     @pl.loop(1, groups)
     def _(k):
         window_copy(W_E, pack.at[0], obs, k).wait_send()
-
-    send_states(S_LOW, *pieces_of[S_LOW])
+        state_copy(S_LOW, *pieces_of[S_LOW], k).start()
+
+    state_own(S_LOW, *pieces_of[S_LOW]).start()
     send_middle()
     send_states(S_HIGH, *pieces_of[S_HIGH])
 

time: 305 us -> 311 us (1.020)
  the two profiles are of different devices: /device:TPU:13 before, /device:TPU:7 now
where the time goes in v6:
time: 311 us; the launch traced here: 310 us
  Pallas kernels  306 us (98%)
  local copies, waits for them, and re-layouts  4.61 us (1%)
    pallas_call x1, Pallas kernels, body(): pl.pallas_call(functools.partial(analysis_kernel, (groups, regions, row,...  306 us

profile of v6, /device:TPU:7, one launch (start us, length us, event | category | flops | bytes accessed | tf_op | source)
XLA Modules:
  0.0 310.5 jit_solution(1252977634671904061)
XLA Ops:
  0.0 305.9 %analysis.1 = f32[128,8192]{1,0:T(8,128)} custom-call(s32[1,4,8]{2,1,0:T(4,128)} %bitcast.4, s32[1,2,4]{2,1,0:T(2,128)} %ids_ref.1, s32[1,9]{1,0:T(1,128)} %offsets_ref.1, s32[1,4,64]{2,1,0:T(4,128)} %bitcast.5, f32[128,8192]{1,0:T(8,128)} %background.1, f32[128,4096]{1,0:T(8,128)} %expected_hbm.1, f32[128,4096]{1,0:T(8,128)} %innov_hbm.1, f32[32,128]{1,0:T(8,128)} %bitcast.3), custom_call_target="tpu_custom_call" | custom-call | tf_op jit(solution)/shard_map/analysis/pallas_call | solution.py:885
  305.9 4.6 %copy.10 = f32[128,8192]{1,0:T(8,128)} copy(f32[128,8192]{1,0:T(8,128)} %analysis.1) | data formatting | bytes 8388608
